TPU v7x, 256 devices: a whole 4x4x8 slice. The times are simulated.
256 devices in a mesh: bead: 16 (over x, z_lo), slab: 8 (over y, z_hi), grp: 2 (over core).
Axes of the slice: x: 4, y: 4, z: 8 (z_hi: 2, z_lo: 4; z = z_hi * 4 + z_lo), core: 2. Of those that a mesh axis runs over, the one named last changes fastest.
Arguments:
- positions: float32 [64, 3, 65536], P('bead', None, ('slab', 'grp')), may hold values from -6 to 6
- momenta: float32 [64, 3, 65536], P('bead', None, ('slab', 'grp')), may hold values from -12 to 12
- force_old: float32 [64, 3, 65536], P('bead', None, ('slab', 'grp')), may hold values from -6 to 6
- noise: float32 [64, 3, 65536], P('bead', None, ('slab', 'grp')), may hold values from -6 to 6
- mass: float32 [65536], P(('slab', 'grp')), may hold values from 1 to 16
- pair_list: int32 [65536, 32], P(('slab', 'grp')), may hold values from 0 to 4351, as said below
- desc_w: bfloat16 [128, 1600], replicated, may hold values from -0.5 to 0.5
- hidden_one: bfloat16 [1600, 240], replicated, may hold values from -0.15625 to 0.15625
- hidden_two: bfloat16 [240, 240], replicated, may hold values from -0.375 to 0.375
- hidden_three: bfloat16 [240, 240], replicated, may hold values from -0.375 to 0.375
- out_w: bfloat16 [240, 3], replicated, may hold values from -0.375 to 0.375
Outputs:
- new_positions: float32 [64, 3, 65536], P('bead', None, ('slab', 'grp'))
- new_momenta: float32 [64, 3, 65536], P('bead', None, ('slab', 'grp'))
- force_new: float32 [64, 3, 65536], P('bead', None, ('slab', 'grp'))
Inputs may be any that keep to these rules, and one draw needn't show every extreme that they name: `pair_list`: for the atom with index li in its slab, every entry lies in li .. li + 256; entries past a count of 16 to 32 per atom name the atom itself, li + 128.
All inputs are finite; a program needn't handle non-finite values.
Results may differ from a plain program's by a relative error of at most 0.00096.
Values sent between devices are 32-bit elements; how exact they have to be, the bound alone decides.
A program may use at most 128 MiB of HBM per device.

v0:
```python
import math

import jax
import jax.numpy as jnp
from jax import lax
from jax.sharding import PartitionSpec as P

BEADS = 64
NC = 8
EDGE = 128


TIME_STEP = 0.1
CYCLE_FREQ = 5.0
CENTROID_FRICTION = 1.0
PAIR_STRENGTH = 0.5


def padded(shard, sides, width):
    for axis, dim in sides:
        count, length = (lax.axis_size(axis), shard.shape[dim])
        up = [(i, (i + 1) % count) for i in range(count)]
        down = [(j, i) for i, j in up]
        last = lax.slice_in_dim(shard, length - width, length, axis=dim)
        first = lax.slice_in_dim(shard, 0, width, axis=dim)
        before = lax.ppermute(last, axis, up)
        after = lax.ppermute(first, axis, down)
        shard = jnp.concatenate([before, shard, after], axis=dim)
    return shard


def cycle_tables(beads, contracted):
    index = jnp.arange(beads, dtype=jnp.float32)
    mode_int = jnp.arange(beads, dtype=jnp.int32)[None, :]
    angle = 2.0 * jnp.pi * index[:, None] * index[None, :] / beads
    half_mode = beads // 2
    root_one = 1.0 / jnp.sqrt(jnp.float32(beads))
    root_two = jnp.sqrt(2.0 / jnp.float32(beads))
    basis = jnp.where(
        mode_int == 0,
        root_one * jnp.ones_like(angle),
        jnp.where(
            mode_int < half_mode,
            root_two * jnp.cos(angle),
            jnp.where(mode_int == half_mode, root_one * jnp.cos(angle), root_two * jnp.sin(angle)),
        ),
    )
    freq = 2.0 * CYCLE_FREQ * jnp.sin(jnp.pi * index / beads)
    cindex = jnp.arange(contracted, dtype=jnp.float32)
    spacing = index[None, :] / beads - cindex[:, None] / contracted
    kernel = jnp.ones_like(spacing)
    for order in range(1, contracted // 2):
        kernel = kernel + 2.0 * jnp.cos(2.0 * jnp.pi * order * spacing)
    kernel = kernel + jnp.cos(jnp.pi * contracted * spacing)
    return (basis, freq, kernel / beads)


def free_drift(modes_q, modes_p, freq, masses):
    step = 0.5 * TIME_STEP
    rate = freq[:, None, None]
    moving = rate > 0.0
    safe = jnp.where(moving, rate, 1.0)
    cosine = jnp.cos(safe * step)
    sine = jnp.sin(safe * step)
    new_q = jnp.where(
        moving,
        cosine * modes_q + sine / (masses * safe) * modes_p,
        modes_q + step * modes_p / masses,
    )
    new_p = jnp.where(moving, cosine * modes_p - masses * safe * sine * modes_q, modes_p)
    return (new_q, new_p)


def thermostat(modes_p, noise, freq, masses):
    friction = jnp.where(freq > 0.0, 2.0 * freq, CENTROID_FRICTION)
    keep = jnp.exp(-friction * TIME_STEP)[:, None, None]
    return keep * modes_p + jnp.sqrt(masses) * jnp.sqrt(1.0 - keep * keep) * noise


def banded_take(extended, lists, start):
    copies = extended.shape[0]
    count, width = lists.shape
    block = math.gcd(count, 128)
    span = block + 2 * EDGE
    flat = extended.reshape(copies * 3, extended.shape[2])
    columns = jnp.arange(span, dtype=jnp.int32)[:, None]

    def one_block(number):
        first = start + number * block
        window = lax.dynamic_slice_in_dim(flat, first, span, 1)
        rows = lax.dynamic_slice_in_dim(lists, number * block, block, 0) - first
        selector = (rows.reshape(1, block * width) == columns).astype(jnp.float32)
        picked = jnp.dot(
            window, selector, precision=lax.Precision.HIGHEST, preferred_element_type=jnp.float32
        )
        return picked.reshape(copies, 3, block, width)

    pieces = lax.map(one_block, jnp.arange(count // block, dtype=jnp.int32))
    return jnp.transpose(pieces, (1, 2, 0, 3, 4)).reshape(copies, 3, count, width)


def contracted_forces(extended, lists, start, weights):
    desc_w, hidden_one, hidden_two, hidden_three, out_w = weights
    count = lists.shape[0]
    copies = extended.shape[0]
    near = banded_take(extended, lists, start)
    own = lax.dynamic_slice_in_dim(extended, start + EDGE, count, 2)[:, :, :, None]
    apart = near - own
    closeness = 1.0 / (1.0 + jnp.sum(apart * apart, axis=1))
    env = jnp.concatenate([apart, closeness[:, None]], axis=1)
    env = jnp.transpose(env, (0, 2, 3, 1)).reshape(copies * count, -1).astype(jnp.bfloat16)
    layer = jnp.tanh(jnp.dot(env, desc_w, preferred_element_type=jnp.float32)).astype(jnp.bfloat16)
    for matrix in (hidden_one, hidden_two, hidden_three):
        layer = jnp.tanh(jnp.dot(layer, matrix, preferred_element_type=jnp.float32)).astype(
            jnp.bfloat16
        )
    output = jnp.dot(layer, out_w, preferred_element_type=jnp.float32)
    return jnp.transpose(output.reshape(copies, count, 3), (0, 2, 1))


def pair_forces(extended, lists):
    count = lists.shape[0]
    near = banded_take(extended, lists, jnp.int32(0))
    own = extended[:, :, EDGE : EDGE + count][:, :, :, None]
    apart = near - own
    closeness = 1.0 / (1.0 + jnp.sum(apart * apart, axis=1, keepdims=True))
    return PAIR_STRENGTH * jnp.sum(apart * closeness, axis=3)


def slab_edges(field):
    return padded(field, ((("slab", "grp"), 2),), EDGE)


def body(
    positions,
    momenta,
    force_old,
    noise,
    mass,
    pair_list,
    desc_w,
    hidden_one,
    hidden_two,
    hidden_three,
    out_w,
):
    best = lax.Precision.HIGHEST
    beads_local = positions.shape[0]
    slab_atoms = positions.shape[2]
    groups = lax.axis_size("bead")
    block_rows = slab_atoms // groups
    place = lax.axis_index("bead")
    start = place * block_rows
    basis, freq, contract = cycle_tables(BEADS, NC)
    weights = (desc_w, hidden_one, hidden_two, hidden_three, out_w)
    ratio = BEADS / NC
    kicked = momenta + 0.5 * TIME_STEP * force_old
    gathered_q, gathered_p, mode_noise = (
        lax.all_to_all(positions, "bead", split_axis=2, concat_axis=0, tiled=True),
        lax.all_to_all(kicked, "bead", split_axis=2, concat_axis=0, tiled=True),
        lax.all_to_all(noise, "bead", split_axis=2, concat_axis=0, tiled=True),
    )
    masses = lax.dynamic_slice_in_dim(mass, start, block_rows, 0)[None, None, :]
    modes_q = jnp.einsum("bk,bxa->kxa", basis, gathered_q, precision=best)
    modes_p = jnp.einsum("bk,bxa->kxa", basis, gathered_p, precision=best)
    modes_q, modes_p = free_drift(modes_q, modes_p, freq, masses)
    modes_p = thermostat(modes_p, mode_noise, freq, masses)
    modes_q, modes_p = free_drift(modes_q, modes_p, freq, masses)
    block_q = jnp.einsum("bk,kxa->bxa", basis, modes_q, precision=best)
    block_p = jnp.einsum("bk,kxa->bxa", basis, modes_p, precision=best)
    row_lists = lax.dynamic_slice_in_dim(pair_list, start, block_rows, 0)
    local_contract = lax.dynamic_slice_in_dim(contract, place * beads_local, beads_local, 1)
    new_q, moved = (
        lax.all_to_all(block_q, "bead", split_axis=0, concat_axis=2, tiled=True),
        lax.all_to_all(block_p, "bead", split_axis=0, concat_axis=2, tiled=True),
    )
    bead_terms = jnp.einsum("cb,bxa->cxa", local_contract, new_q, precision=best)
    slab_contracted = lax.psum(bead_terms, "bead")
    neural = contracted_forces(slab_edges(slab_contracted), row_lists, start, weights)
    spread = ratio * jnp.einsum(
        "cb,cxa->bxa",
        local_contract,
        lax.all_gather(neural, "bead", axis=2, tiled=True),
        precision=best,
    )
    bead_extended = padded(new_q, ((("slab", "grp"), 2),), EDGE)
    pairs = pair_forces(bead_extended, pair_list)
    force_new = pairs + spread
    return (new_q, moved + 0.5 * TIME_STEP * force_new, force_new)


def solution(mesh):
    placed = (
        P("bead", None, ("slab", "grp")),
        P("bead", None, ("slab", "grp")),
        P("bead", None, ("slab", "grp")),
        P("bead", None, ("slab", "grp")),
        P(("slab", "grp")),
        P(("slab", "grp"), None),
        P(),
        P(),
        P(),
        P(),
        P(),
    )
    return jax.shard_map(
        body,
        mesh=mesh,
        in_specs=placed,
        out_specs=(
            P("bead", None, ("slab", "grp")),
            P("bead", None, ("slab", "grp")),
            P("bead", None, ("slab", "grp")),
        ),
        check_vma=False,
    )
```

profile of v0, /device:TPU:0, one launch (start us, length us, event | category | flops | bytes accessed | tf_op | source)
XLA Modules:
  0.0 457.1 jit_solution(15007762217400926848)
XLA Ops:
  7.2 6.7 %copy.125 = f32[4,3,4096]{0,1,2:T(4,128)} copy(f32[4,3,4096]{2,0,1:T(4,128)} %param.18) | data formatting | bytes 393216 | tf_op args[3]
  13.9 8.9 %reshape.263 = f32[16,1,3072]{2,1,0:T(1,128)} reshape(f32[4096,3,4]{2,1,0:T(4,128)} %bitcast.121) | data formatting | bytes 393216
  22.8 6.8 %all-to-all-start.2 = ((f32[16,1,3072]{2,1,0:T(1,128)}), f32[16,1,3072]{2,1,0:T(1,128)S(1)}, u32[]{:S(2)}, u32[]{:S(2)}) async-start(f32[16,1,3072]{2,1,0:T(1,128)} %reshape.263), calls=%async_computation.2 | async-start | bytes 393216 | tf_op jit(solution)/shard_map/all_to_all | solution.py:161
  29.8 6.0 %copy.119 = f32[4,3,4096]{0,1,2:T(4,128)} copy(f32[4,3,4096]{2,0,1:T(4,128)S(1)} %copy-done.5) | data formatting | bytes 393216 | tf_op args[0]
  35.7 8.9 %reshape.267 = f32[16,1,3072]{2,1,0:T(1,128)} reshape(f32[4096,3,4]{2,1,0:T(4,128)} %bitcast.122) | data formatting | bytes 393216
  44.9 7.5 %all-to-all-start = ((f32[16,1,3072]{2,1,0:T(1,128)}), f32[16,1,3072]{2,1,0:T(1,128)S(1)}, u32[]{:S(2)}, u32[]{:S(2)}) async-start(f32[16,1,3072]{2,1,0:T(1,128)} %reshape.267), calls=%async_computation | async-start | bytes 393216 | tf_op jit(solution)/shard_map/all_to_all | solution.py:159
  52.5 6.0 %copy.122 = f32[4,3,4096]{0,1,2:T(4,128)} copy(f32[4,3,4096]{2,0,1:T(4,128)S(1)} %multiply_add_fusion.2) | data formatting | bytes 393216 | tf_op jit(solution)/shard_map/add | solution.py:157
  58.4 8.9 %reshape.265 = f32[16,1,3072]{2,1,0:T(1,128)} reshape(f32[4096,3,4]{2,1,0:T(4,128)} %bitcast.117) | data formatting | bytes 393216
  67.5 8.0 %all-to-all-start.1 = ((f32[16,1,3072]{2,1,0:T(1,128)}), f32[16,1,3072]{2,1,0:T(1,128)S(1)}, u32[]{:S(2)}, u32[]{:S(2)}) async-start(f32[16,1,3072]{2,1,0:T(1,128)} %reshape.265), calls=%async_computation.1 | async-start | bytes 393216 | tf_op jit(solution)/shard_map/all_to_all | solution.py:160
  78.0 7.2 %reshape.264 = f32[4096,3,4]{2,1,0:T(4,128)} reshape(f32[16,3072]{1,0:T(8,128)S(1)} %reduce.3) | data formatting | bytes 393216
  85.2 6.5 %copy.126 = f32[4,3,16,256]{3,0,2,1:T(4,128)S(1)} copy(f32[4,3,16,256]{0,1,3,2:T(4,128)} %bitcast.118) | data formatting | bytes 393216 | tf_op jit(solution)/shard_map/all_to_all | solution.py:161
  92.9 7.2 %reshape.268 = f32[4096,3,4]{2,1,0:T(4,128)} reshape(f32[16,3072]{1,0:T(8,128)S(1)} %reduce.4) | data formatting | bytes 393216
  100.1 6.5 %copy.120 = f32[4,3,16,256]{3,0,2,1:T(4,128)S(1)} copy(f32[4,3,16,256]{0,1,3,2:T(4,128)} %bitcast.119) | data formatting | bytes 393216 | tf_op jit(solution)/shard_map/all_to_all | solution.py:159
  107.8 7.2 %reshape.266 = f32[4096,3,4]{2,1,0:T(4,128)} reshape(f32[16,3072]{1,0:T(8,128)S(1)} %reduce.5) | data formatting | bytes 393216
  115.0 6.6 %copy.123 = f32[4,3,16,256]{3,0,2,1:T(4,128)S(1)} copy(f32[4,3,16,256]{0,1,3,2:T(4,128)} %bitcast.120) | data formatting | bytes 393216 | tf_op jit(solution)/shard_map/all_to_all | solution.py:160
  124.3 7.6 %all-to-all-start.3 = ((f32[64,3,256]{2,1,0:T(4,128)}), f32[64,3,256]{2,1,0:T(4,128)S(1)}, u32[]{:S(2)}, u32[]{:S(2)}) async-start(f32[64,3,256]{2,1,0:T(4,128)} %copy.127), calls=%async_computation.3 | async-start | bytes 524288 | tf_op jit(solution)/shard_map/all_to_all | solution.py:174
  136.4 4.6 %all-to-all-done.3 = f32[64,3,256]{2,1,0:T(4,128)S(1)} async-done(((f32[64,3,256]{2,1,0:T(4,128)}), f32[64,3,256]{2,1,0:T(4,128)S(1)}, u32[]{:S(2)}, u32[]{:S(2)}) %all-to-all-start.3) | async-done | bytes 196640 | tf_op jit(solution)/shard_map/all_to_all | solution.py:174
  141.0 3.7 all-to-all-start.4
  145.0 3.4 collective-permute-start.1
  149.9 3.9 all-to-all-done.4
  154.5 3.0 collective-permute-done
  157.6 173.7 %while.22 = (s32[]{:T(128)}, f32[32,4,3,128,32]{4,3,2,1,0:T(8,128)}, s32[32]{0:T(128)S(1)}, f32[12,4352]{1,0:T(8,128)S(1)}, s32[4096,32]{1,0:T(8,128)}, /*index=...) while((s32[]{:T(128)}, f32[32,4,3,128,32]{4,3,2,1,0:T(8,128)}, s32[32]{0:T(128)S(1)}, ...), condition=%wide.region_1.2_spmd.clone, body=%wide.region_0.1_spmd.clone.sunk | while | flops 228069376 | bytes 1679568 | solution.py:98
  159.8 2.0 fusion.127
  165.2 2.0 fusion.127
  170.6 2.0 fusion.127
  176.1 2.0 fusion.127
  181.5 2.0 fusion.127
  186.9 2.0 fusion.127
  192.3 2.0 fusion.127
  241.2 2.0 fusion.127
  252.0 2.0 fusion.127
  279.2 2.0 fusion.127
  290.0 2.0 fusion.127
  295.4 2.0 fusion.127
  300.8 2.0 fusion.127
  306.2 2.0 fusion.127
  322.5 2.0 fusion.127
  331.2 14.3 %multiply_reduce_fusion.1 = f32[4,32,128,32]{3,2,0,1:T(8,128)} fusion(f32[32,4,3,128,32]{4,3,2,1,0:T(8,128)} %get-tuple-element.72, f32[4,3,32,128]{3,1,0,2:T(4,128)S(1)} %copy.135), kind=kLoop, calls=%fused_computation.18 | loop fusion | flops 4194304 | bytes 8585216 | tf_op jit(solution)/shard_map/reduce_sum | solution.py:126
  345.5 4.5 add_divide_fusion
  350.0 16.5 %multiply_reduce_fusion = f32[4,3,32,128]{3,1,0,2:T(4,128)S(1)} fusion(f32[32,4,3,128,32]{4,3,2,1,0:T(8,128)} %get-tuple-element.72, f32[4,32,128,32]{3,2,0,1:T(8,128)S(1)} %add_divide_fusion, f32[4,3,32,128]{3,1,0,2:T(4,128)S(1)} %copy.135), kind=kLoop, calls=%fused_computation.17 | loop fusion | flops 4669440 | bytes 8781824 | tf_op jit(solution)/shard_map/reduce_sum | solution.py:127
  367.4 8.0 %collective-permute-start.3 = (f32[8,3,128]{2,0,1:T(8,128)S(1)}, f32[8,3,128]{2,0,1:T(8,128)S(1)}, u32[]{:S(2)}, u32[]{:S(2)}) collective-permute-start(f32[8,3,128]{2,0,1:T(8,128)S(1)} %get-tuple-element.149), channel_id=1, source_target_pairs={{1,0},{2,1},{3,2},{4,3},{5,4},{6,5},{7,6},{8,7},{9,8},{10,9},{11,1... | collective-permute-start | bytes 36872 | tf_op jit(solution)/shard_map/ppermute | solution.py:27
  378.7 11.8 %while.23 = (s32[]{:T(128)}, f32[2,8,3,128,32]{4,3,2,1,0:T(8,128)}, s32[2]{0:T(128)S(1)}, s32[]{:T(128)}, f32[24,4352]{1,0:T(8,128)}, /*index=5*/s32[256,32]{1,0...) while((s32[]{:T(128)}, f32[2,8,3,128,32]{4,3,2,1,0:T(8,128)}, ...), condition=%wide.region_6.7_spmd.clone, body=%wide.region_5.6_spmd.clone.sunk | while | flops 454561792 | bytes 3264749 | solution.py:98
  380.1 2.8 fusion.129
  386.0 2.8 fusion.129
  390.6 2.5 multiply_reduce_fusion.2
  393.6 2.4 copy.141
  397.3 4.6 %fusion.15 = bf16[2048,240]{0,1:T(8,128)(2,1)S(1)} fusion(bf16[1600,240]{0,1:T(8,128)(2,1)S(1)} %copy-done, bf16[128,1600]{0,1:T(8,128)(2,1)} %param.21, bf16[2048,128]{0,1:T(8,128)(2,1)S(1)} %bitcast.138), kind=kOutput, calls=%fused_computation.28 | convolution fusion | flops 2415493120 | bytes 2684928 | tf_op jit(solution)/shard_map/dot_general | solution.py:114
  403.0 45.6 %all_gather.3 = f32[8,3,4096]{2,0,1:T(8,128)S(1)} all-gather(f32[8,3,256]{2,0,1:T(8,128)S(1)} %bitcast.140), channel_id=1, replica_groups=mesh['bead'=16,'slab'=8,'grp'=2] {'bead'}, dimensions={2}, use_global_device_ids=true | all-gather | bytes 417792 | tf_op jit(solution)/shard_map/all_gather | solution.py:183
  (291 shorter events, 150.8 us)
Async XLA Ops:
  7.2 390.1 %copy-start = (bf16[1600,240]{0,1:T(8,128)(2,1)S(1)}, bf16[1600,240]{0,1:T(8,128)(2,1)}, u32[]{:S(2)}) copy-start(bf16[1600,240]{0,1:T(8,128)(2,1)} %param.22) | copy-start | bytes 2304004
  7.2 22.4 %copy-start.3 = (f32[4,3,4096]{2,0,1:T(4,128)S(1)}, f32[4,3,4096]{2,0,1:T(4,128)}, u32[]{:S(2)}) copy-start(f32[4,3,4096]{2,0,1:T(4,128)} %param.16) | copy-start | bytes 589828
  7.2 22.4 %copy-start.4 = (f32[4,3,4096]{2,0,1:T(4,128)S(1)}, f32[4,3,4096]{2,0,1:T(4,128)}, u32[]{:S(2)}) copy-start(f32[4,3,4096]{2,0,1:T(4,128)} %param.17) | copy-start | bytes 589828
  7.2 22.6 %copy-start.5 = (f32[4,3,4096]{2,0,1:T(4,128)S(1)}, f32[4,3,4096]{2,0,1:T(4,128)}, u32[]{:S(2)}) copy-start(f32[4,3,4096]{2,0,1:T(4,128)} %param.15) | copy-start | bytes 589828
  22.8 22.1 %all-to-all-start.2 = ((f32[16,1,3072]{2,1,0:T(1,128)}), f32[16,1,3072]{2,1,0:T(1,128)S(1)}, u32[]{:S(2)}, u32[]{:S(2)}) async-start(f32[16,1,3072]{2,1,0:T(1,128)} %reshape.263), calls=%async_computation.2 | async-start | bytes 393216 | tf_op jit(solution)/shard_map/all_to_all | solution.py:161
  44.9 22.5 %all-to-all-start = ((f32[16,1,3072]{2,1,0:T(1,128)}), f32[16,1,3072]{2,1,0:T(1,128)S(1)}, u32[]{:S(2)}, u32[]{:S(2)}) async-start(f32[16,1,3072]{2,1,0:T(1,128)} %reshape.267), calls=%async_computation | async-start | bytes 393216 | tf_op jit(solution)/shard_map/all_to_all | solution.py:159
  67.5 39.2 %all-to-all-start.1 = ((f32[16,1,3072]{2,1,0:T(1,128)}), f32[16,1,3072]{2,1,0:T(1,128)S(1)}, u32[]{:S(2)}, u32[]{:S(2)}) async-start(f32[16,1,3072]{2,1,0:T(1,128)} %reshape.265), calls=%async_computation.1 | async-start | bytes 393216 | tf_op jit(solution)/shard_map/all_to_all | solution.py:160
  115.0 17.1 %copy-start.2 = (s32[4096,32]{0,1:T(8,128)S(1)}, s32[4096,32]{0,1:T(8,128)}, u32[]{:S(2)}) copy-start(s32[4096,32]{0,1:T(8,128)} %param.20) | copy-start | bytes 1572868
  124.3 16.7 %all-to-all-start.3 = ((f32[64,3,256]{2,1,0:T(4,128)}), f32[64,3,256]{2,1,0:T(4,128)S(1)}, u32[]{:S(2)}, u32[]{:S(2)}) async-start(f32[64,3,256]{2,1,0:T(4,128)} %copy.127), calls=%async_computation.3 | async-start | bytes 524288 | tf_op jit(solution)/shard_map/all_to_all | solution.py:174
  141.0 12.8 %all-to-all-start.4 = ((f32[64,3,256]{2,1,0:T(4,128)}), f32[64,3,256]{2,1,0:T(4,128)S(1)}, u32[]{:S(2)}, u32[]{:S(2)}) async-start(f32[64,3,256]{2,1,0:T(4,128)} %copy.130), calls=%async_computation.4 | async-start | bytes 524288 | tf_op jit(solution)/shard_map/all_to_all | solution.py:175
  144.7 221.8 %all-reduce.2.cloned.1.call-start = ((), (), s32[]{:S(2)}) async-start(), calls=%async_computation.5 | async-start | bytes 786432 | tf_op jit(solution)/shard_map/psum | solution.py:178
  145.0 12.5 %copy-start.1 = (f32[4,3,4096]{2,0,1:T(4,128)}, f32[4,3,4096]{2,0,1:T(4,128)S(1)}, u32[]{:S(2)}) copy-start(f32[4,3,4096]{2,0,1:T(4,128)S(1)} %all_to_all.80) | copy-start | bytes 589828
  145.0 9.4 %collective-permute-start.1 = (f32[4,3,128]{2,0,1:T(4,128)S(1)}, f32[4,3,128]{2,0,1:T(4,128)S(1)}, u32[]{:S(2)}, u32[]{:S(2)}) collective-permute-start(f32[4,3,128]{2,0,1:T(4,128)S(1)} %get-tuple-element.152), channel_id=1, source_target_pairs={{1,0},{2,1},{3,2},{4,3},{5,4},{6,5},{7,6},{8,7},{9,8},{10,9},{11,1... | collective-permute-start | bytes 18440 | tf_op jit(solution)/shard_map/ppermute | solution.py:27
  148.4 9.1 %collective-permute-start = (f32[4,3,128]{2,0,1:T(4,128)S(1)}, f32[4,3,128]{2,0,1:T(4,128)S(1)}, u32[]{:S(2)}, u32[]{:S(2)}) collective-permute-start(f32[4,3,128]{2,0,1:T(4,128)S(1)} %get-tuple-element.151), channel_id=1, source_target_pairs={{0,1},{1,2},{2,3},{3,4},{4,5},{5,6},{6,7},{7,8},{8,9},{9,10},{10,1... | collective-permute-start | bytes 18440 | tf_op jit(solution)/shard_map/ppermute | solution.py:26
  367.2 9.1 %collective-permute-start.2 = (f32[8,3,128]{2,0,1:T(8,128)S(1)}, f32[8,3,128]{2,0,1:T(8,128)S(1)}, u32[]{:S(2)}, u32[]{:S(2)}) collective-permute-start(f32[8,3,128]{2,0,1:T(8,128)S(1)} %get-tuple-element.150), channel_id=1, source_target_pairs={{0,1},{1,2},{2,3},{3,4},{4,5},{5,6},{6,7},{7,8},{8,9},{9,10},{10,1... | collective-permute-start | bytes 36872 | tf_op jit(solution)/shard_map/ppermute | solution.py:26
  367.4 10.0 %collective-permute-start.3 = (f32[8,3,128]{2,0,1:T(8,128)S(1)}, f32[8,3,128]{2,0,1:T(8,128)S(1)}, u32[]{:S(2)}, u32[]{:S(2)}) collective-permute-start(f32[8,3,128]{2,0,1:T(8,128)S(1)} %get-tuple-element.149), channel_id=1, source_target_pairs={{1,0},{2,1},{3,2},{4,3},{5,4},{6,5},{7,6},{8,7},{9,8},{10,9},{11,1... | collective-permute-start | bytes 36872 | tf_op jit(solution)/shard_map/ppermute | solution.py:27
  396.0 5.9 %copy-start.6 = (bf16[240,240]{1,0:T(8,128)(2,1)S(1)}, bf16[240,240]{1,0:T(8,128)(2,1)}, u32[]{:S(2)}) copy-start(bf16[240,240]{1,0:T(8,128)(2,1)} %param.23) | copy-start | bytes 345604
  396.8 5.6 %copy-start.7 = (bf16[240,240]{1,0:T(8,128)(2,1)S(1)}, bf16[240,240]{1,0:T(8,128)(2,1)}, u32[]{:S(2)}) copy-start(bf16[240,240]{1,0:T(8,128)(2,1)} %param.24) | copy-start | bytes 345604
  396.8 5.6 %copy-start.8 = (bf16[240,3]{0,1:T(4,128)(2,1)S(1)}, bf16[240,3]{0,1:T(4,128)(2,1)}, u32[]{:S(2)}) copy-start(bf16[240,3]{0,1:T(4,128)(2,1)} %param.25) | copy-start | bytes 4324
Sparse Core Ops, SparseCore 0:
  154.6 160.6 all-reduce.1
where the time goes:
time: 464 us; the launch traced here: 457 us
  local copies, waits for them, and re-layouts  167 us (36%)
  matrix products  81.2 us (18%)
  other arithmetic  69.4 us (15%)
  blocking collectives  45.6 us (10%)
  starting transfers between devices  45 us (10%)
  loops' own time  21.9 us (5%)
  between operations  14.9 us (3%)
  waiting for transfers between devices  12.5 us (3%)
    dot_general x34, matrix products, one_block(): jnp.dot(window, selector, precision=lax.Precision.HIGHEST, preferred_elem...  70.5 us
    unnamed x33, local copies, waits for them, and re-layouts  64.3 us
    all_gather x1, blocking collectives, body(): lax.all_gather(neural, 'bead', axis=2, tiled=True)  45.6 us
    dynamic_update_slice x34, local copies, waits for them, and re-layouts, banded_take(): pieces = lax.map(one_block, jnp.arange(count // block, dtype=jnp.int32))  33.3 us
    sub x34, other arithmetic, one_block(): rows = lax.dynamic_slice_in_dim(lists, number * block, block, 0) - first  27.3 us
    another operation x2, loops' own time, banded_take(): pieces = lax.map(one_block, jnp.arange(count // block, dtype=jnp.int32))  21.9 us
    dynamic_slice x34, local copies, waits for them, and re-layouts, banded_take(): pieces = lax.map(one_block, jnp.arange(count // block, dtype=jnp.int32))  21.5 us
    reduce_sum x1, other arithmetic, pair_forces(): return PAIR_STRENGTH * jnp.sum(apart * closeness, axis=3)  16.5 us
  transfers between devices with their start and end apart: 10, of which 4 were waited for; matrix products, arithmetic and copies ran while one was open for 56% of the time, Pallas kernels for 0%

commit v1 on v0

v1 whole, which is shorter than its diff:
```python
import functools

import jax
import jax.numpy as jnp
import numpy as np
from jax import lax
from jax.experimental import pallas as pl
from jax.experimental.pallas import tpu as pltpu
from jax.sharding import PartitionSpec as P

BEADS = 64
NC = 8
LANE = 128
TIME_STEP = 0.1
CYCLE_FREQ = 5.0
CENTROID_FRICTION = 1.0
PAIR_STRENGTH = 0.5
MESH = pl.DeviceIdType.MESH


def cycle_tables(beads, contracted):
    index = np.arange(beads, dtype=np.float64)
    mode = np.arange(beads)[None, :]
    angle = 2.0 * np.pi * index[:, None] * index[None, :] / beads
    half = beads // 2
    root_one = 1.0 / np.sqrt(beads)
    root_two = np.sqrt(2.0 / beads)
    alternate = np.where(np.arange(beads) % 2 == 0, 1.0, -1.0)[:, None]
    basis = np.where(
        mode == 0,
        root_one,
        np.where(
            mode < half,
            root_two * np.cos(angle),
            np.where(mode == half, root_one * alternate, root_two * np.sin(angle)),
        ),
    )
    freq = 2.0 * CYCLE_FREQ * np.sin(np.pi * index / beads)
    spacing = index[None, :] / beads - np.arange(contracted)[:, None] / contracted
    kernel = np.ones_like(spacing)
    for order in range(1, contracted // 2):
        kernel = kernel + 2.0 * np.cos(2.0 * np.pi * order * spacing)
    kernel = kernel + np.cos(np.pi * contracted * spacing)
    return basis, freq, kernel / beads


def step_tables(beads, contracted):
    basis, freq, contract = cycle_tables(beads, contracted)
    step = 0.5 * TIME_STEP
    moving = freq > 0.0
    safe = np.where(moving, freq, 1.0)
    cos = np.where(moving, np.cos(safe * step), 1.0)
    sin_over = np.where(moving, np.sin(safe * step) / safe, step)
    sin_times = np.where(moving, np.sin(safe * step) * safe, 0.0)
    keep = np.exp(-np.where(moving, 2.0 * freq, CENTROID_FRICTION) * TIME_STEP)
    kick = np.sqrt(1.0 - keep * keep)

    def both(diag):
        return (basis * diag[None, :]) @ basis.T

    q_rows = np.concatenate(
        [
            both(cos * cos - keep * sin_over * sin_times),
            both(cos * sin_over * (1.0 + keep)),
            basis * (sin_over * kick)[None, :],
        ],
        axis=1,
    )
    p_rows = np.concatenate(
        [
            both(-cos * sin_times * (1.0 + keep)),
            both(cos * cos * keep - sin_over * sin_times),
            basis * (cos * kick)[None, :],
        ],
        axis=1,
    )
    return np.concatenate([q_rows, p_rows, contract @ q_rows], axis=0), contract


def split_table(table):
    table = jnp.asarray(table.astype(np.float32))
    high = table.astype(jnp.bfloat16)
    low = (table - high.astype(jnp.float32)).astype(jnp.bfloat16)
    return high, low


def dot32(left, right):
    return jnp.dot(left, right, preferred_element_type=jnp.float32)


def table_dot(high, low, x):
    x_high = x.astype(jnp.bfloat16)
    x_low = (x - x_high.astype(jnp.float32)).astype(jnp.bfloat16)
    return dot32(high, x_high) + (dot32(high, x_low) + dot32(low, x_high))


def near_minus_own(rows, low, first, third):
    got = [
        jnp.take_along_axis(
            jnp.broadcast_to(row, low.shape), low, axis=1, mode="promise_in_bounds"
        )
        for row in rows
    ]
    near = jnp.where(first, got[0], jnp.where(third, got[2], got[1]))
    return near - rows[1]


def tile_lists(list_ref, tile):
    index = list_ref[:, pl.ds(pl.multiple_of(tile * LANE, LANE), LANE)] - tile * LANE
    return index & (LANE - 1), index < LANE, index >= 2 * LANE


def kernel(
    groups,
    q_hbm,
    n_hbm,
    p_hbm,
    f_hbm,
    mass_hbm,
    list_hbm,
    desc_hbm,
    one_hbm,
    two_hbm,
    three_hbm,
    out_w_hbm,
    perm_hbm,
    w_high_hbm,
    w_low_hbm,
    s_high_hbm,
    s_low_hbm,
    out_q,
    out_m,
    out_f,
    p_ref,
    f_ref,
    mass_ref,
    two_ref,
    three_ref,
    out_w_ref,
    perm_ref,
    w_high,
    w_low,
    s_high,
    s_low,
    kick_buf,
    recv_in,
    xs,
    y_buf,
    back,
    ext,
    neural,
    s_buf,
    s_recv,
    pair_buf,
    lists,
    desc,
    desc_p,
    one,
    local_sem,
    own_sem,
    in_send,
    in_recv,
    y_send,
    y_recv,
    s_send,
    s_recv_sem,
    halo_send,
    halo_recv,
    edge_send,
    edge_recv,
):
    nb = groups
    bl = p_ref.shape[1]
    last = p_ref.shape[2]
    block = p_ref.shape[2] // nb
    tiles = p_ref.shape[2] // LANE
    wide = block // LANE
    beads = nb * bl
    nc = ext.shape[1]
    me = lax.axis_index("bead")
    slabs, cores = lax.axis_size("slab"), lax.axis_size("grp")
    total = slabs * cores
    slab = lax.axis_index("slab") * cores + lax.axis_index("grp")

    def device(place, at):
        return {"bead": place, "slab": at // cores, "grp": at % cores}

    up, down = (slab + 1) % total, (slab + total - 1) % total
    after = device((me + 1) % nb, (slab + (me + 1) // nb) % total)
    before = device((me + nb - 1) % nb, (slab + total - 1 + (me + nb - 1) // nb) % total)

    moves = (
        (p_hbm, p_ref),
        (f_hbm, f_ref),
        (desc_hbm, desc),
        (perm_hbm, perm_ref),
        (mass_hbm, mass_ref),
        (w_high_hbm, w_high),
        (w_low_hbm, w_low),
        (list_hbm, lists),
        (one_hbm, one),
        (two_hbm, two_ref),
        (three_hbm, three_ref),
        (out_w_hbm, out_w_ref),
        (s_high_hbm, s_high),
        (s_low_hbm, s_low),
    )
    loads = [
        pltpu.make_async_copy(source, dest, local_sem.at[at])
        for at, (source, dest) in enumerate(moves)
    ]
    for load in loads:
        load.start()

    barrier = pltpu.get_barrier_semaphore()

    def greet(off, carry):
        pl.semaphore_signal(
            barrier, inc=1, device_id=device((me + off) % nb, slab), device_id_type=MESH
        )
        return carry

    lax.fori_loop(1, nb, greet, 0)
    for other in (device(me, up), device(me, down), before, after):
        pl.semaphore_signal(barrier, inc=1, device_id=other, device_id_type=MESH)
    for load in loads[:2]:
        load.wait()
    kick_buf[...] = p_ref[...] + 0.5 * TIME_STEP * f_ref[...]
    pl.semaphore_wait(barrier, nb - 1 + 4)

    def lanes_of(place):
        return pl.ds(pl.multiple_of(place * block, LANE), block)

    sources = (q_hbm, n_hbm, kick_buf)

    def send_in(which, dest, source):
        return pltpu.make_async_remote_copy(
            src_ref=sources[which].at[:, :, lanes_of(dest)],
            dst_ref=recv_in.at[which, source],
            send_sem=in_send.at[which, dest],
            recv_sem=in_recv.at[which, source],
            device_id=device(dest, slab),
            device_id_type=MESH,
        )

    def start_in(off, carry):
        for which in range(3):
            send_in(which, (me + off) % nb, me).start()
        return carry

    lax.fori_loop(1, nb, start_in, 0)
    owns = [
        pltpu.make_async_copy(
            sources[which].at[:, :, lanes_of(me)], recv_in.at[which, me], own_sem.at[which]
        )
        for which in range(3)
    ]
    for own in owns:
        own.start()

    for load in loads[2:]:
        load.wait()
    desc_p[...] = dot32(desc[...], perm_ref[...]).astype(jnp.bfloat16)

    for own in owns:
        own.wait()

    def wait_in(off, carry):
        for which in range(3):
            send_in(which, (me + off) % nb, (me + off) % nb).wait_recv()
        return carry

    lax.fori_loop(1, nb, wait_in, 0)

    for which, part in ((0, 0), (2, 1), (1, 2)):
        for place in range(nb):
            for comp in range(3):
                row = part * beads + place * bl
                xs[row : row + bl, comp * block : (comp + 1) * block] = recv_in[which, place, comp]
    heavy = jnp.concatenate(
        [mass_ref[pl.ds(me * wide + h, 1), :] for h in range(wide)] * 3, axis=1
    )
    x_all = jnp.concatenate(
        [
            xs[0:beads, :],
            xs[beads : 2 * beads, :] / heavy,
            xs[2 * beads : 3 * beads, :] / jnp.sqrt(heavy),
        ],
        axis=0,
    )
    y_all = table_dot(w_high[...], w_low[...], x_all)
    contracted = y_all[2 * beads : 2 * beads + nc]
    for comp in range(3):
        for cb in range(nc):
            ext[comp, cb, :, LANE : LANE + block] = contracted[
                cb : cb + 1, comp * block : (comp + 1) * block
            ]
    y_new = y_all[0:beads]
    y_mom = y_all[beads : 2 * beads] * heavy
    for arr, value in ((0, y_new), (1, y_mom)):
        for place in range(nb):
            for comp in range(3):
                y_buf[arr, place, comp] = value[
                    place * bl : (place + 1) * bl, comp * block : (comp + 1) * block
                ]

    far = LANE + block
    halos = [
        pltpu.make_async_remote_copy(
            src_ref=ext.at[:, :, :, pl.ds(block, LANE)],
            dst_ref=ext.at[:, :, :, pl.ds(0, LANE)],
            send_sem=halo_send.at[0],
            recv_sem=halo_recv.at[0],
            device_id=after,
            device_id_type=MESH,
        ),
        pltpu.make_async_remote_copy(
            src_ref=ext.at[:, :, :, pl.ds(LANE, LANE)],
            dst_ref=ext.at[:, :, :, pl.ds(far, LANE)],
            send_sem=halo_send.at[1],
            recv_sem=halo_recv.at[1],
            device_id=before,
            device_id_type=MESH,
        ),
    ]
    for halo in halos:
        halo.start()

    def back_lanes(source):
        return pl.ds(pl.multiple_of(LANE + source * block, LANE), block)

    def send_y(arr, dest, source):
        return pltpu.make_async_remote_copy(
            src_ref=y_buf.at[arr, dest],
            dst_ref=back.at[arr, :, :, back_lanes(source)],
            send_sem=y_send.at[arr, dest],
            recv_sem=y_recv.at[arr, source],
            device_id=device(dest, slab),
            device_id_type=MESH,
        )

    for arr in range(2):

        def start_y(off, carry, arr=arr):
            send_y(arr, (me + off) % nb, me).start()
            return carry

        lax.fori_loop(1, nb, start_y, 0)
    y_own = [
        pltpu.make_async_copy(
            y_buf.at[arr, me], back.at[arr, :, :, back_lanes(me)], own_sem.at[arr]
        )
        for arr in range(2)
    ]
    for own in y_own:
        own.start()
    for halo in halos:
        halo.wait_recv()

    chunk = 512
    depth = one.shape[1]

    def one_contracted(cb, carry):
        env = []
        for h in range(wide):
            low, first, third = tile_lists(lists, me * wide + h)
            apart = []
            for comp in range(3):
                rows = [
                    ext[comp, cb, :, (h + k) * LANE : (h + k + 1) * LANE] for k in range(3)
                ]
                apart.append(near_minus_own(rows, low, first, third))
            close = 1.0 / (
                1.0 + (apart[0] * apart[0] + apart[1] * apart[1] + apart[2] * apart[2])
            )
            env.append(jnp.concatenate(apart + [close], axis=0).astype(jnp.bfloat16))
        env = jnp.concatenate(env, axis=1)
        total_one = None
        for low_at in range(0, depth, chunk):
            high_at = min(low_at + chunk, depth)
            piece = jnp.tanh(dot32(desc_p[low_at:high_at, :], env)).astype(jnp.bfloat16)
            term = dot32(one[:, low_at:high_at], piece)
            total_one = term if total_one is None else total_one + term
        layer = jnp.tanh(total_one).astype(jnp.bfloat16)
        for matrix in (two_ref, three_ref):
            layer = jnp.tanh(
                lax.dot_general(
                    matrix[...],
                    layer,
                    (((0,), (0,)), ((), ())),
                    preferred_element_type=jnp.float32,
                )
            ).astype(jnp.bfloat16)
        force = dot32(out_w_ref[...], layer)
        neural[cb] = force
        return carry

    lax.fori_loop(0, nc, one_contracted, 0)

    for comp in range(3):
        rows = jnp.concatenate([neural[cb, comp : comp + 1, :] for cb in range(nc)], axis=0)
        spread = table_dot(s_high[...], s_low[...], rows)
        for place in range(nb):
            s_buf[place, comp] = spread[place * bl : (place + 1) * bl, :]

    def send_s(dest, source):
        return pltpu.make_async_remote_copy(
            src_ref=s_buf.at[dest],
            dst_ref=s_recv.at[:, :, lanes_of(source)],
            send_sem=s_send.at[dest],
            recv_sem=s_recv_sem.at[source],
            device_id=device(dest, slab),
            device_id_type=MESH,
        )

    def start_s(off, carry):
        send_s((me + off) % nb, me).start()
        return carry

    lax.fori_loop(1, nb, start_s, 0)
    s_own = pltpu.make_async_copy(s_buf.at[me], s_recv.at[:, :, lanes_of(me)], own_sem.at[2])
    s_own.start()

    for own in y_own:
        own.wait()
    for arr in range(2):

        def wait_y(off, carry, arr=arr):
            send_y(arr, (me + off) % nb, (me + off) % nb).wait_recv()
            return carry

        lax.fori_loop(1, nb, wait_y, 0)

    edges = [
        pltpu.make_async_remote_copy(
            src_ref=back.at[0, :, :, pl.ds(last, LANE)],
            dst_ref=back.at[0, :, :, pl.ds(0, LANE)],
            send_sem=edge_send.at[0],
            recv_sem=edge_recv.at[0],
            device_id=device(me, up),
            device_id_type=MESH,
        ),
        pltpu.make_async_remote_copy(
            src_ref=back.at[0, :, :, pl.ds(LANE, LANE)],
            dst_ref=back.at[0, :, :, pl.ds(last + LANE, LANE)],
            send_sem=edge_send.at[1],
            recv_sem=edge_recv.at[1],
            device_id=device(me, down),
            device_id_type=MESH,
        ),
    ]
    for edge in edges:
        edge.start()

    def one_tile(tile, carry):
        low, first, third = tile_lists(lists, tile)
        at = [pl.ds(pl.multiple_of((tile + k) * LANE, LANE), LANE) for k in range(3)]
        sums = [[], [], []]
        for bead in range(bl):
            apart = []
            for comp in range(3):
                rows = [back[0, comp, bead : bead + 1, at[k]] for k in range(3)]
                apart.append(near_minus_own(rows, low, first, third))
            close = PAIR_STRENGTH / (
                1.0 + (apart[0] * apart[0] + apart[1] * apart[1] + apart[2] * apart[2])
            )
            for comp in range(3):
                sums[comp].append(jnp.sum(apart[comp] * close, axis=0, keepdims=True))
        for comp in range(3):
            pair_buf[comp, :, at[0]] = jnp.concatenate(sums[comp], axis=0)
        return carry

    lax.fori_loop(1, tiles - 1, one_tile, 0)
    for edge in edges:
        edge.wait_recv()

    def outer_tile(which, carry):
        return one_tile(which * (tiles - 1), carry)

    lax.fori_loop(0, 2, outer_tile, 0)

    s_own.wait()

    def wait_s(off, carry):
        send_s((me + off) % nb, (me + off) % nb).wait_recv()
        return carry

    lax.fori_loop(1, nb, wait_s, 0)
    force = pair_buf[...] + s_recv[...]
    out_f[...] = force
    out_m[...] = back[1, :, :, LANE : LANE + last] + 0.5 * TIME_STEP * force
    out_q[...] = back[0, :, :, LANE : LANE + last]

    def drain(off, carry):
        dest = (me + off) % nb
        for which in range(3):
            send_in(which, dest, me).wait_send()
        for arr in range(2):
            send_y(arr, dest, me).wait_send()
        send_s(dest, me).wait_send()
        return carry

    lax.fori_loop(1, nb, drain, 0)
    for copy in halos + edges:
        copy.wait_send()


def body(
    positions,
    momenta,
    force_old,
    noise,
    mass,
    pair_list,
    desc_w,
    hidden_one,
    hidden_two,
    hidden_three,
    out_w,
):
    nb = lax.axis_size("bead")
    bl, _, atoms = positions.shape
    beads = nb * bl
    block = atoms // nb
    width = pair_list.shape[1]
    env, wide = desc_w.shape
    hid = hidden_one.shape[1]
    table, contract = step_tables(beads, NC)
    w_high, w_low = split_table(table)
    s_high, s_low = split_table(contract.T * (beads / NC))
    perm = np.zeros((env, env), np.float32)
    for j in range(width):
        for entry in range(4):
            perm[4 * j + entry, entry * width + j] = 1.0
    perm = jnp.asarray(perm, jnp.bfloat16)

    def flip(x):
        return jnp.transpose(x, (1, 0, 2))

    out = jax.ShapeDtypeStruct((3, bl, atoms), jnp.float32)
    f32, bf16 = jnp.float32, jnp.bfloat16
    dma = pltpu.SemaphoreType.DMA
    new_q, new_m, new_f = pl.pallas_call(
        functools.partial(kernel, nb),
        out_shape=(out, out, out),
        in_specs=[pl.BlockSpec(memory_space=pltpu.HBM)] * 16,
        out_specs=(pl.BlockSpec(memory_space=pltpu.VMEM),) * 3,
        scratch_shapes=[
            pltpu.VMEM((3, bl, atoms), f32),
            pltpu.VMEM((3, bl, atoms), f32),
            pltpu.VMEM((atoms // LANE, LANE), f32),
            pltpu.VMEM((hid, hid), bf16),
            pltpu.VMEM((hid, hid), bf16),
            pltpu.VMEM((3, hid), bf16),
            pltpu.VMEM((env, env), bf16),
            pltpu.VMEM(w_high.shape, bf16),
            pltpu.VMEM(w_low.shape, bf16),
            pltpu.VMEM(s_high.shape, bf16),
            pltpu.VMEM(s_low.shape, bf16),
            pltpu.VMEM((3, bl, atoms), f32),
            pltpu.VMEM((3, nb, 3, bl, block), f32),
            pltpu.VMEM((3 * beads, 3 * block), f32),
            pltpu.VMEM((2, nb, 3, bl, block), f32),
            pltpu.VMEM((2, 3, bl, atoms + 2 * LANE), f32),
            pltpu.VMEM((3, NC, 1, block + 2 * LANE), f32),
            pltpu.VMEM((NC, 3, block), f32),
            pltpu.VMEM((nb, 3, bl, block), f32),
            pltpu.VMEM((3, bl, atoms), f32),
            pltpu.VMEM((3, bl, atoms), f32),
            pltpu.VMEM((width, atoms), jnp.int32),
            pltpu.VMEM((wide, env), bf16),
            pltpu.VMEM((wide, env), bf16),
            pltpu.VMEM((hid, wide), bf16),
            dma((14,)),
            dma((3,)),
            dma((3, nb)),
            dma((3, nb)),
            dma((2, nb)),
            dma((2, nb)),
            dma((nb,)),
            dma((nb,)),
            dma((2,)),
            dma((2,)),
            dma((2,)),
            dma((2,)),
        ],
        compiler_params=pltpu.CompilerParams(
            collective_id=0, has_side_effects=True, vmem_limit_bytes=66519040
        ),
    )(
        flip(positions),
        flip(noise),
        flip(momenta),
        flip(force_old),
        mass.reshape(atoms // LANE, LANE),
        pair_list.T,
        desc_w.T,
        hidden_one.T,
        hidden_two,
        hidden_three,
        out_w.T,
        perm,
        w_high,
        w_low,
        s_high,
        s_low,
    )
    return flip(new_q), flip(new_m), flip(new_f)


def solution(mesh):
    whole = P("bead", None, ("slab", "grp"))
    placed = (whole,) * 4 + (P(("slab", "grp")), P(("slab", "grp"), None)) + (P(),) * 5
    return jax.shard_map(
        body, mesh=mesh, in_specs=placed, out_specs=(whole,) * 3, check_vma=False
    )
```

time: 464 us -> 67.7 us (0.15)
  the two profiles are of different devices: /device:TPU:0 before, /device:TPU:1 now
where the time goes in v1:
time: 67.7 us; the launch traced here: 67.5 us
  Pallas kernels  63.5 us (94%)
  local copies, waits for them, and re-layouts  3.33 us (5%)
    pallas_call x1, Pallas kernels, body(): pl.pallas_call(functools.partial(kernel, nb), out_shape=(out, out, out),...  63.5 us
    unnamed x7, local copies, waits for them, and re-layouts  3.33 us

profile of v1, /device:TPU:1, one launch (start us, length us, event | category | flops | bytes accessed | tf_op | source)
XLA Modules:
  0.0 67.5 jit_solution(1719483517042719382)
XLA Ops:
  0.6 63.5 %shard_map.157 = (f32[3,4,4096]{2,1,0:T(4,128)}, f32[3,4,4096]{2,1,0:T(4,128)}, f32[3,4,4096]{2,1,0:T(4,128)}) custom-call(f32[3,4,4096]{2,1,0:T(4,128)} %bitcast.15, f32[3,4,4096]{2,1,0:T(4,128)} %bitcast.16, f32[3,4,4096]{2,1,0:T(4,128)} %bitcast.17, f32[3,4,4096]{2,1,0:T(4,128)} %bitcast.18, f32[32,128]{1,0:T(8,128)} %bitcast.22, s32[32,4096]{1,0:T(8,128)} %bitcast.13, ...), custom_call_target="tpu_custom_call" | custom-call | tf_op jit(solution)/shard_map/pallas_call | solution.py:543
  64.1 0.0 copy-start.1
  64.1 1.7 %copy.20 = f32[4,3,4096]{2,0,1:T(4,128)} copy(f32[4,3,4096]{2,0,1:T(4,128)} %bitcast.21) | data formatting | bytes 393216
  65.8 0.0 copy-done.1
  65.8 0.0 copy-start
  65.8 0.7 %copy.21 = f32[4,3,4096]{2,0,1:T(4,128)} copy(f32[4,3,4096]{2,0,1:T(4,128)S(1)} %bitcast.20) | data formatting | bytes 393216
  66.5 0.3 copy-done
  66.8 0.7 %copy.22 = f32[4,3,4096]{2,0,1:T(4,128)} copy(f32[4,3,4096]{2,0,1:T(4,128)S(1)} %bitcast.19) | data formatting | bytes 393216
Async XLA Ops:
  64.1 1.7 %copy-start.1 = (f32[3,4,4096]{2,1,0:T(4,128)S(1)}, f32[3,4,4096]{2,1,0:T(4,128)}, u32[]{:S(2)}) copy-start(f32[3,4,4096]{2,1,0:T(4,128)} %get-tuple-element.7) | copy-start | bytes 589828
  65.8 1.0 %copy-start = (f32[3,4,4096]{2,1,0:T(4,128)S(1)}, f32[3,4,4096]{2,1,0:T(4,128)}, u32[]{:S(2)}) copy-start(f32[3,4,4096]{2,1,0:T(4,128)} %get-tuple-element.8) | copy-start | bytes 589828

commit v2 on v1

--- a/solution.py
+++ b/solution.py
@@ -94,20 +94,24 @@
     return dot32(high, x_high) + (dot32(high, x_low) + dot32(low, x_high))
 
 
-def near_minus_own(rows, low, first, third):
+def gather_near(rows, low, first, third):
     got = [
         jnp.take_along_axis(
             jnp.broadcast_to(row, low.shape), low, axis=1, mode="promise_in_bounds"
         )
         for row in rows
     ]
-    near = jnp.where(first, got[0], jnp.where(third, got[2], got[1]))
-    return near - rows[1]
-
-
-def tile_lists(list_ref, tile):
-    index = list_ref[:, pl.ds(pl.multiple_of(tile * LANE, LANE), LANE)] - tile * LANE
+    return jnp.where(first, got[0], jnp.where(third, got[2], got[1])) - rows[1]
+
+
+def tile_lists(list_ref, tile, group):
+    lanes = pl.ds(pl.multiple_of(tile * LANE, LANE), LANE)
+    index = list_ref[8 * group : 8 * group + 8, lanes] - tile * LANE
     return index & (LANE - 1), index < LANE, index >= 2 * LANE
+
+
+def closeness(apart, scale):
+    return scale / (1.0 + (apart[0] * apart[0] + apart[1] * apart[1] + apart[2] * apart[2]))
 
 
 def kernel(
@@ -156,6 +160,9 @@
     desc,
     desc_p,
     one,
+    two_t,
+    three_t,
+    env_buf,
     local_sem,
     own_sem,
     in_send,
@@ -186,8 +193,33 @@
         return {"bead": place, "slab": at // cores, "grp": at % cores}
 
     up, down = (slab + 1) % total, (slab + total - 1) % total
-    after = device((me + 1) % nb, (slab + (me + 1) // nb) % total)
-    before = device((me + nb - 1) % nb, (slab + total - 1 + (me + nb - 1) // nb) % total)
+
+    def block_of(place, at=slab):
+        if nb != 16:
+            return place
+        core, shift = at % cores, (3 * (at // cores)) % 4
+        x, z = (place // 4 + 4 - shift) % 4, place % 4
+        along_x = 4 * z + x + (z % 2) * (3 - 2 * x)
+        along_z = 4 * x + 3 - z + (x % 2) * (2 * z - 3)
+        return along_x + core * (along_z - along_x)
+
+    def place_of(number, at):
+        if nb != 16:
+            return number
+        core, shift = at % cores, (3 * (at // cores)) % 4
+        far, near = number // 4, number % 4
+        x_first = 4 * ((near + (far % 2) * (3 - 2 * near) + shift) % 4) + far
+        z_first = 4 * ((far + shift) % 4) + 3 - near + (far % 2) * (2 * near - 3)
+        return x_first + core * (z_first - x_first)
+
+    mine = block_of(me)
+
+    def beside(step):
+        number = mine + step + nb
+        at = (slab + total + number // nb - 1) % total
+        return device(place_of(number % nb, at), at)
+
+    after, before = beside(1), beside(-1)
 
     moves = (
         (p_hbm, p_ref),
@@ -229,7 +261,7 @@
     pl.semaphore_wait(barrier, nb - 1 + 4)
 
     def lanes_of(place):
-        return pl.ds(pl.multiple_of(place * block, LANE), block)
+        return pl.ds(pl.multiple_of(block_of(place) * block, LANE), block)
 
     sources = (q_hbm, n_hbm, kick_buf)
 
@@ -261,6 +293,8 @@
     for load in loads[2:]:
         load.wait()
     desc_p[...] = dot32(desc[...], perm_ref[...]).astype(jnp.bfloat16)
+    two_t[...] = jnp.transpose(two_ref[...])
+    three_t[...] = jnp.transpose(three_ref[...])
 
     for own in owns:
         own.wait()
@@ -278,7 +312,7 @@
                 row = part * beads + place * bl
                 xs[row : row + bl, comp * block : (comp + 1) * block] = recv_in[which, place, comp]
     heavy = jnp.concatenate(
-        [mass_ref[pl.ds(me * wide + h, 1), :] for h in range(wide)] * 3, axis=1
+        [mass_ref[pl.ds(mine * wide + h, 1), :] for h in range(wide)] * 3, axis=1
     )
     x_all = jnp.concatenate(
         [
@@ -327,7 +361,7 @@
         halo.start()
 
     def back_lanes(source):
-        return pl.ds(pl.multiple_of(LANE + source * block, LANE), block)
+        return pl.ds(pl.multiple_of(LANE + block_of(source) * block, LANE), block)
 
     def send_y(arr, dest, source):
         return pltpu.make_async_remote_copy(
@@ -357,24 +391,37 @@
     for halo in halos:
         halo.wait_recv()
 
+    width = lists.shape[0]
+    for h in range(wide):
+        for pair in range(width // 16):
+            picks = [tile_lists(lists, mine * wide + h, 2 * pair + k) for k in range(2)]
+            for cb in range(nc):
+                halves = []
+                for low, first, third in picks:
+                    apart = []
+                    for comp in range(3):
+                        rows = [
+                            ext[comp, cb, :, (h + k) * LANE : (h + k + 1) * LANE]
+                            for k in range(3)
+                        ]
+                        apart.append(gather_near(rows, low, first, third))
+                    halves.append(apart + [closeness(apart, 1.0)])
+                for entry in range(4):
+                    at = entry * width + 16 * pair
+                    env_buf[
+                        cb // 2,
+                        at : at + 16,
+                        ((cb % 2) * wide + h) * LANE : ((cb % 2) * wide + h + 1) * LANE,
+                    ] = (
+                        jnp.concatenate([halves[0][entry], halves[1][entry]], axis=0).astype(
+                            jnp.bfloat16
+                        )
+                    )
     chunk = 512
     depth = one.shape[1]
 
-    def one_contracted(cb, carry):
-        env = []
-        for h in range(wide):
-            low, first, third = tile_lists(lists, me * wide + h)
-            apart = []
-            for comp in range(3):
-                rows = [
-                    ext[comp, cb, :, (h + k) * LANE : (h + k + 1) * LANE] for k in range(3)
-                ]
-                apart.append(near_minus_own(rows, low, first, third))
-            close = 1.0 / (
-                1.0 + (apart[0] * apart[0] + apart[1] * apart[1] + apart[2] * apart[2])
-            )
-            env.append(jnp.concatenate(apart + [close], axis=0).astype(jnp.bfloat16))
-        env = jnp.concatenate(env, axis=1)
+    def two_contracted(step, carry):
+        env = env_buf[step]
         total_one = None
         for low_at in range(0, depth, chunk):
             high_at = min(low_at + chunk, depth)
@@ -382,23 +429,18 @@
             term = dot32(one[:, low_at:high_at], piece)
             total_one = term if total_one is None else total_one + term
         layer = jnp.tanh(total_one).astype(jnp.bfloat16)
-        for matrix in (two_ref, three_ref):
-            layer = jnp.tanh(
-                lax.dot_general(
-                    matrix[...],
-                    layer,
-                    (((0,), (0,)), ((), ())),
-                    preferred_element_type=jnp.float32,
-                )
-            ).astype(jnp.bfloat16)
-        force = dot32(out_w_ref[...], layer)
-        neural[cb] = force
-        return carry
-
-    lax.fori_loop(0, nc, one_contracted, 0)
+        for matrix in (two_t, three_t):
+            layer = jnp.tanh(dot32(matrix[...], layer)).astype(jnp.bfloat16)
+        neural[step] = dot32(out_w_ref[...], layer)
+        return carry
+
+    lax.fori_loop(0, nc // 2, two_contracted, 0)
 
     for comp in range(3):
-        rows = jnp.concatenate([neural[cb, comp : comp + 1, :] for cb in range(nc)], axis=0)
+        rows = jnp.concatenate([
+                neural[cb // 2, comp : comp + 1, (cb % 2) * block : (cb % 2 + 1) * block]
+                for cb in range(nc)
+            ], axis=0)
         spread = table_dot(s_high[...], s_low[...], rows)
         for place in range(nb):
             s_buf[place, comp] = spread[place * bl : (place + 1) * bl, :]
@@ -453,24 +495,32 @@
         edge.start()
 
     def one_tile(tile, carry):
-        low, first, third = tile_lists(lists, tile)
         at = [pl.ds(pl.multiple_of((tile + k) * LANE, LANE), LANE) for k in range(3)]
-        sums = [[], [], []]
-        for bead in range(bl):
-            apart = []
-            for comp in range(3):
-                rows = [back[0, comp, bead : bead + 1, at[k]] for k in range(3)]
-                apart.append(near_minus_own(rows, low, first, third))
-            close = PAIR_STRENGTH / (
-                1.0 + (apart[0] * apart[0] + apart[1] * apart[1] + apart[2] * apart[2])
+        sums = [[None] * bl for _ in range(3)]
+        for group in range(width // 8):
+            low, first, third = tile_lists(lists, tile, group)
+            for bead in range(bl):
+                apart = []
+                for comp in range(3):
+                    rows = [back[0, comp, bead : bead + 1, at[k]] for k in range(3)]
+                    apart.append(gather_near(rows, low, first, third))
+                close = closeness(apart, PAIR_STRENGTH)
+                for comp in range(3):
+                    term = apart[comp] * close
+                    old = sums[comp][bead]
+                    sums[comp][bead] = term if old is None else old + term
+        for comp in range(3):
+            pair_buf[comp, :, at[0]] = jnp.concatenate(
+                [jnp.sum(part, axis=0, keepdims=True) for part in sums[comp]], axis=0
             )
-            for comp in range(3):
-                sums[comp].append(jnp.sum(apart[comp] * close, axis=0, keepdims=True))
-        for comp in range(3):
-            pair_buf[comp, :, at[0]] = jnp.concatenate(sums[comp], axis=0)
-        return carry
-
-    lax.fori_loop(1, tiles - 1, one_tile, 0)
+        return carry
+
+    def inner_tiles(step, carry):
+        for k in range(2):
+            one_tile(1 + 2 * step + k, carry)
+        return carry
+
+    lax.fori_loop(0, (tiles - 2) // 2, inner_tiles, 0)
     for edge in edges:
         edge.wait_recv()
 
@@ -563,7 +613,7 @@
             pltpu.VMEM((2, nb, 3, bl, block), f32),
             pltpu.VMEM((2, 3, bl, atoms + 2 * LANE), f32),
             pltpu.VMEM((3, NC, 1, block + 2 * LANE), f32),
-            pltpu.VMEM((NC, 3, block), f32),
+            pltpu.VMEM((NC // 2, 3, 2 * block), f32),
             pltpu.VMEM((nb, 3, bl, block), f32),
             pltpu.VMEM((3, bl, atoms), f32),
             pltpu.VMEM((3, bl, atoms), f32),
@@ -571,6 +621,9 @@
             pltpu.VMEM((wide, env), bf16),
             pltpu.VMEM((wide, env), bf16),
             pltpu.VMEM((hid, wide), bf16),
+            pltpu.VMEM((hid, hid), bf16),
+            pltpu.VMEM((hid, hid), bf16),
+            pltpu.VMEM((NC // 2, env, 2 * block), bf16),
             dma((14,)),
             dma((3,)),
             dma((3, nb)),

time: 67.7 us -> 51.4 us (0.76)
  the two profiles are of different devices: /device:TPU:1 before, /device:TPU:8 now
where the time goes in v2:
time: 51.4 us; the launch traced here: 51.2 us
  Pallas kernels  47.2 us (92%)
  local copies, waits for them, and re-layouts  3.33 us (6%)
  between operations  0.65 us (1%)
    pallas_call x1, Pallas kernels, body(): pl.pallas_call(functools.partial(kernel, nb), out_shape=(out, out, out),...  47.2 us
    unnamed x7, local copies, waits for them, and re-layouts  3.33 us

profile of v2, /device:TPU:8, one launch (start us, length us, event | category | flops | bytes accessed | tf_op | source)
XLA Modules:
  0.0 51.2 jit_solution(1036279441010013547)
XLA Ops:
  0.6 47.2 %shard_map.157 = (f32[3,4,4096]{2,1,0:T(4,128)}, f32[3,4,4096]{2,1,0:T(4,128)}, f32[3,4,4096]{2,1,0:T(4,128)}) custom-call(f32[3,4,4096]{2,1,0:T(4,128)} %bitcast.15, f32[3,4,4096]{2,1,0:T(4,128)} %bitcast.16, f32[3,4,4096]{2,1,0:T(4,128)} %bitcast.17, f32[3,4,4096]{2,1,0:T(4,128)} %bitcast.18, f32[32,128]{1,0:T(8,128)} %bitcast.22, s32[32,4096]{1,0:T(8,128)} %bitcast.13, ...), custom_call_target="tpu_custom_call" | custom-call | tf_op jit(solution)/shard_map/pallas_call | solution.py:593
  47.8 0.0 copy-start.1
  47.9 1.7 %copy.20 = f32[4,3,4096]{2,0,1:T(4,128)} copy(f32[4,3,4096]{2,0,1:T(4,128)} %bitcast.21) | data formatting | bytes 393216
  49.5 0.0 copy-done.1
  49.5 0.0 copy-start
  49.5 0.7 %copy.21 = f32[4,3,4096]{2,0,1:T(4,128)} copy(f32[4,3,4096]{2,0,1:T(4,128)S(1)} %bitcast.20) | data formatting | bytes 393216
  50.2 0.3 copy-done
  50.5 0.7 %copy.22 = f32[4,3,4096]{2,0,1:T(4,128)} copy(f32[4,3,4096]{2,0,1:T(4,128)S(1)} %bitcast.19) | data formatting | bytes 393216
Async XLA Ops:
  47.8 1.7 %copy-start.1 = (f32[3,4,4096]{2,1,0:T(4,128)S(1)}, f32[3,4,4096]{2,1,0:T(4,128)}, u32[]{:S(2)}) copy-start(f32[3,4,4096]{2,1,0:T(4,128)} %get-tuple-element.7) | copy-start | bytes 589828
  49.5 1.0 %copy-start = (f32[3,4,4096]{2,1,0:T(4,128)S(1)}, f32[3,4,4096]{2,1,0:T(4,128)}, u32[]{:S(2)}) copy-start(f32[3,4,4096]{2,1,0:T(4,128)} %get-tuple-element.8) | copy-start | bytes 589828

commit v3 on v2

--- a/solution.py
+++ b/solution.py
@@ -146,7 +146,7 @@
     w_low,
     s_high,
     s_low,
-    kick_buf,
+    sent,
     recv_in,
     xs,
     y_buf,
@@ -163,6 +163,7 @@
     two_t,
     three_t,
     env_buf,
+    layer_buf,
     local_sem,
     own_sem,
     in_send,
@@ -224,6 +225,8 @@
     moves = (
         (p_hbm, p_ref),
         (f_hbm, f_ref),
+        (q_hbm, sent.at[0]),
+        (n_hbm, sent.at[2]),
         (desc_hbm, desc),
         (perm_hbm, perm_ref),
         (mass_hbm, mass_ref),
@@ -255,62 +258,51 @@
     lax.fori_loop(1, nb, greet, 0)
     for other in (device(me, up), device(me, down), before, after):
         pl.semaphore_signal(barrier, inc=1, device_id=other, device_id_type=MESH)
-    for load in loads[:2]:
+    for load in loads[:4]:
         load.wait()
-    kick_buf[...] = p_ref[...] + 0.5 * TIME_STEP * f_ref[...]
+    sent[1] = p_ref[...] + 0.5 * TIME_STEP * f_ref[...]
     pl.semaphore_wait(barrier, nb - 1 + 4)
 
     def lanes_of(place):
         return pl.ds(pl.multiple_of(block_of(place) * block, LANE), block)
 
-    sources = (q_hbm, n_hbm, kick_buf)
-
-    def send_in(which, dest, source):
+    def send_in(dest, source):
         return pltpu.make_async_remote_copy(
-            src_ref=sources[which].at[:, :, lanes_of(dest)],
-            dst_ref=recv_in.at[which, source],
-            send_sem=in_send.at[which, dest],
-            recv_sem=in_recv.at[which, source],
+            src_ref=sent.at[:, :, :, lanes_of(dest)],
+            dst_ref=recv_in.at[source],
+            send_sem=in_send.at[dest],
+            recv_sem=in_recv.at[source],
             device_id=device(dest, slab),
             device_id_type=MESH,
         )
 
     def start_in(off, carry):
-        for which in range(3):
-            send_in(which, (me + off) % nb, me).start()
+        send_in((me + off) % nb, me).start()
         return carry
 
     lax.fori_loop(1, nb, start_in, 0)
-    owns = [
-        pltpu.make_async_copy(
-            sources[which].at[:, :, lanes_of(me)], recv_in.at[which, me], own_sem.at[which]
-        )
-        for which in range(3)
-    ]
-    for own in owns:
-        own.start()
-
-    for load in loads[2:]:
+    own_in = pltpu.make_async_copy(sent.at[:, :, :, lanes_of(me)], recv_in.at[me], own_sem.at[0])
+    own_in.start()
+
+    for load in loads[4:]:
         load.wait()
     desc_p[...] = dot32(desc[...], perm_ref[...]).astype(jnp.bfloat16)
     two_t[...] = jnp.transpose(two_ref[...])
     three_t[...] = jnp.transpose(three_ref[...])
 
-    for own in owns:
-        own.wait()
+    own_in.wait()
 
     def wait_in(off, carry):
-        for which in range(3):
-            send_in(which, (me + off) % nb, (me + off) % nb).wait_recv()
+        send_in((me + off) % nb, (me + off) % nb).wait_recv()
         return carry
 
     lax.fori_loop(1, nb, wait_in, 0)
 
-    for which, part in ((0, 0), (2, 1), (1, 2)):
+    for part in range(3):
         for place in range(nb):
             for comp in range(3):
                 row = part * beads + place * bl
-                xs[row : row + bl, comp * block : (comp + 1) * block] = recv_in[which, place, comp]
+                xs[row : row + bl, comp * block : (comp + 1) * block] = recv_in[place, part, comp]
     heavy = jnp.concatenate(
         [mass_ref[pl.ds(mine * wide + h, 1), :] for h in range(wide)] * 3, axis=1
     )
@@ -334,7 +326,7 @@
     for arr, value in ((0, y_new), (1, y_mom)):
         for place in range(nb):
             for comp in range(3):
-                y_buf[arr, place, comp] = value[
+                y_buf[place, arr, comp] = value[
                     place * bl : (place + 1) * bl, comp * block : (comp + 1) * block
                 ]
 
@@ -363,31 +355,23 @@
     def back_lanes(source):
         return pl.ds(pl.multiple_of(LANE + block_of(source) * block, LANE), block)
 
-    def send_y(arr, dest, source):
+    def send_y(dest, source):
         return pltpu.make_async_remote_copy(
-            src_ref=y_buf.at[arr, dest],
-            dst_ref=back.at[arr, :, :, back_lanes(source)],
-            send_sem=y_send.at[arr, dest],
-            recv_sem=y_recv.at[arr, source],
+            src_ref=y_buf.at[dest],
+            dst_ref=back.at[:, :, :, back_lanes(source)],
+            send_sem=y_send.at[dest],
+            recv_sem=y_recv.at[source],
             device_id=device(dest, slab),
             device_id_type=MESH,
         )
 
-    for arr in range(2):
-
-        def start_y(off, carry, arr=arr):
-            send_y(arr, (me + off) % nb, me).start()
-            return carry
-
-        lax.fori_loop(1, nb, start_y, 0)
-    y_own = [
-        pltpu.make_async_copy(
-            y_buf.at[arr, me], back.at[arr, :, :, back_lanes(me)], own_sem.at[arr]
-        )
-        for arr in range(2)
-    ]
-    for own in y_own:
-        own.start()
+    def start_y(off, carry):
+        send_y((me + off) % nb, me).start()
+        return carry
+
+    lax.fori_loop(1, nb, start_y, 0)
+    y_own = pltpu.make_async_copy(y_buf.at[me], back.at[:, :, :, back_lanes(me)], own_sem.at[1])
+    y_own.start()
     for halo in halos:
         halo.wait_recv()
 
@@ -428,13 +412,15 @@
             piece = jnp.tanh(dot32(desc_p[low_at:high_at, :], env)).astype(jnp.bfloat16)
             term = dot32(one[:, low_at:high_at], piece)
             total_one = term if total_one is None else total_one + term
-        layer = jnp.tanh(total_one).astype(jnp.bfloat16)
-        for matrix in (two_t, three_t):
-            layer = jnp.tanh(dot32(matrix[...], layer)).astype(jnp.bfloat16)
+        layer_buf[step] = jnp.tanh(total_one).astype(jnp.bfloat16)
+        return carry
+
+    lax.fori_loop(0, nc // 2, two_contracted, 0)
+    layers = [layer_buf[step] for step in range(nc // 2)]
+    for matrix in (two_t, three_t):
+        layers = [jnp.tanh(dot32(matrix[...], layer)).astype(jnp.bfloat16) for layer in layers]
+    for step, layer in enumerate(layers):
         neural[step] = dot32(out_w_ref[...], layer)
-        return carry
-
-    lax.fori_loop(0, nc // 2, two_contracted, 0)
 
     for comp in range(3):
         rows = jnp.concatenate([
@@ -463,15 +449,13 @@
     s_own = pltpu.make_async_copy(s_buf.at[me], s_recv.at[:, :, lanes_of(me)], own_sem.at[2])
     s_own.start()
 
-    for own in y_own:
-        own.wait()
-    for arr in range(2):
-
-        def wait_y(off, carry, arr=arr):
-            send_y(arr, (me + off) % nb, (me + off) % nb).wait_recv()
-            return carry
-
-        lax.fori_loop(1, nb, wait_y, 0)
+    y_own.wait()
+
+    def wait_y(off, carry):
+        send_y((me + off) % nb, (me + off) % nb).wait_recv()
+        return carry
+
+    lax.fori_loop(1, nb, wait_y, 0)
 
     edges = [
         pltpu.make_async_remote_copy(
@@ -515,12 +499,14 @@
             )
         return carry
 
+    together = next(n for n in (5, 3, 2, 1) if (tiles - 2) % n == 0)
+
     def inner_tiles(step, carry):
-        for k in range(2):
-            one_tile(1 + 2 * step + k, carry)
-        return carry
-
-    lax.fori_loop(0, (tiles - 2) // 2, inner_tiles, 0)
+        for k in range(together):
+            one_tile(1 + together * step + k, carry)
+        return carry
+
+    lax.fori_loop(0, (tiles - 2) // together, inner_tiles, 0)
     for edge in edges:
         edge.wait_recv()
 
@@ -543,10 +529,8 @@
 
     def drain(off, carry):
         dest = (me + off) % nb
-        for which in range(3):
-            send_in(which, dest, me).wait_send()
-        for arr in range(2):
-            send_y(arr, dest, me).wait_send()
+        send_in(dest, me).wait_send()
+        send_y(dest, me).wait_send()
         send_s(dest, me).wait_send()
         return carry
 
@@ -607,10 +591,10 @@
             pltpu.VMEM(w_low.shape, bf16),
             pltpu.VMEM(s_high.shape, bf16),
             pltpu.VMEM(s_low.shape, bf16),
-            pltpu.VMEM((3, bl, atoms), f32),
-            pltpu.VMEM((3, nb, 3, bl, block), f32),
+            pltpu.VMEM((3, 3, bl, atoms), f32),
+            pltpu.VMEM((nb, 3, 3, bl, block), f32),
             pltpu.VMEM((3 * beads, 3 * block), f32),
-            pltpu.VMEM((2, nb, 3, bl, block), f32),
+            pltpu.VMEM((nb, 2, 3, bl, block), f32),
             pltpu.VMEM((2, 3, bl, atoms + 2 * LANE), f32),
             pltpu.VMEM((3, NC, 1, block + 2 * LANE), f32),
             pltpu.VMEM((NC // 2, 3, 2 * block), f32),
@@ -624,12 +608,13 @@
             pltpu.VMEM((hid, hid), bf16),
             pltpu.VMEM((hid, hid), bf16),
             pltpu.VMEM((NC // 2, env, 2 * block), bf16),
-            dma((14,)),
+            pltpu.VMEM((NC // 2, hid, 2 * block), bf16),
+            dma((16,)),
             dma((3,)),
-            dma((3, nb)),
-            dma((3, nb)),
-            dma((2, nb)),
-            dma((2, nb)),
+            dma((nb,)),
+            dma((nb,)),
+            dma((nb,)),
+            dma((nb,)),
             dma((nb,)),
             dma((nb,)),
             dma((2,)),
@@ -638,9 +623,10 @@
             dma((2,)),
         ],
         compiler_params=pltpu.CompilerParams(
-            collective_id=0, has_side_effects=True, vmem_limit_bytes=66519040
+            collective_id=0, has_side_effects=True, vmem_limit_bytes=50331648
         ),
-    )(
+    )(*[pltpu.with_memory_space_constraint(x, pltpu.HBM) for x in (
+
         flip(positions),
         flip(noise),
         flip(momenta),
@@ -657,7 +643,7 @@
         w_low,
         s_high,
         s_low,
-    )
+        )])
     return flip(new_q), flip(new_m), flip(new_f)
 
 

time: 51.4 us -> 46 us (0.89)
  the two profiles are of different devices: /device:TPU:8 before, /device:TPU:1 now
where the time goes in v3:
time: 46 us; the launch traced here: 45.9 us
  Pallas kernels  43.2 us (94%)
  local copies, waits for them, and re-layouts  2.03 us (4%)
  between operations  0.64 us (1%)
    pallas_call x1, Pallas kernels, body(): pl.pallas_call(functools.partial(kernel, nb), out_shape=(out, out, out),...  43.2 us
    unnamed x3, local copies, waits for them, and re-layouts  2.03 us

profile of v3, /device:TPU:1, one launch (start us, length us, event | category | flops | bytes accessed | tf_op | source)
XLA Modules:
  0.0 45.9 jit_solution(3146292775206109892)
XLA Ops:
  0.6 43.2 %shard_map.157 = (f32[3,4,4096]{2,1,0:T(4,128)S(1)}, f32[3,4,4096]{2,1,0:T(4,128)S(1)}, f32[3,4,4096]{2,1,0:T(4,128)S(1)}) custom-call(f32[3,4,4096]{2,1,0:T(4,128)} %bitcast.18, f32[3,4,4096]{2,1,0:T(4,128)} %bitcast.19, f32[3,4,4096]{2,1,0:T(4,128)} %bitcast.20, f32[3,4,4096]{2,1,0:T(4,128)} %bitcast.21, f32[32,128]{1,0:T(8,128)} %bitcast.22, ...), custom_call_target="tpu_custom_call" | custom-call | tf_op jit(solution)/shard_map/pallas_call | solution.py:577
  43.8 0.7 %copy.20 = f32[4,3,4096]{2,0,1:T(4,128)} copy(f32[4,3,4096]{2,0,1:T(4,128)S(1)} %bitcast.14) | data formatting | bytes 393216
  44.5 0.7 %copy.21 = f32[4,3,4096]{2,0,1:T(4,128)} copy(f32[4,3,4096]{2,0,1:T(4,128)S(1)} %bitcast.13) | data formatting | bytes 393216
  45.2 0.7 %copy.22 = f32[4,3,4096]{2,0,1:T(4,128)} copy(f32[4,3,4096]{2,0,1:T(4,128)S(1)} %bitcast.12) | data formatting | bytes 393216

commit v4 on v3

--- a/solution.py
+++ b/solution.py
@@ -155,6 +155,7 @@
     neural,
     s_buf,
     s_recv,
+    edge_buf,
     pair_buf,
     lists,
     desc,
@@ -176,6 +177,8 @@
     halo_recv,
     edge_send,
     edge_recv,
+    relay_send,
+    relay_recv,
 ):
     nb = groups
     bl = p_ref.shape[1]
@@ -193,7 +196,6 @@
     def device(place, at):
         return {"bead": place, "slab": at // cores, "grp": at % cores}
 
-    up, down = (slab + 1) % total, (slab + total - 1) % total
 
     def block_of(place, at=slab):
         if nb != 16:
@@ -256,12 +258,12 @@
         return carry
 
     lax.fori_loop(1, nb, greet, 0)
-    for other in (device(me, up), device(me, down), before, after):
+    for other in (before, after):
         pl.semaphore_signal(barrier, inc=1, device_id=other, device_id_type=MESH)
     for load in loads[:4]:
         load.wait()
     sent[1] = p_ref[...] + 0.5 * TIME_STEP * f_ref[...]
-    pl.semaphore_wait(barrier, nb - 1 + 4)
+    pl.semaphore_wait(barrier, nb - 1 + 2)
 
     def lanes_of(place):
         return pl.ds(pl.multiple_of(block_of(place) * block, LANE), block)
@@ -352,6 +354,42 @@
     for halo in halos:
         halo.start()
 
+    ends = ((0, 0), (1, nb - 1))
+
+    def relay(which):
+        return pltpu.make_async_remote_copy(
+            src_ref=y_buf.at[:, 0, :, :, pl.ds((1 - which) * (block - LANE), LANE)],
+            dst_ref=edge_buf.at[which],
+            send_sem=relay_send.at[which],
+            recv_sem=relay_recv.at[which],
+            device_id=(after, before)[which],
+            device_id_type=MESH,
+        )
+
+    def edge_lanes(which):
+        return pl.ds(which * (last + LANE), LANE)
+
+    def hand(which, dest):
+        return pltpu.make_async_remote_copy(
+            src_ref=edge_buf.at[which, dest],
+            dst_ref=back.at[0, :, :, edge_lanes(which)],
+            send_sem=edge_send.at[dest],
+            recv_sem=edge_recv.at[which],
+            device_id=device(dest, slab),
+            device_id_type=MESH,
+        )
+
+    def keep(which):
+        return pltpu.make_async_copy(
+            edge_buf.at[which, me], back.at[0, :, :, edge_lanes(which)], own_sem.at[3 + which]
+        )
+
+    for which, end in ends:
+
+        @pl.when(mine == nb - 1 - end)
+        def _(which=which):
+            relay(which).start()
+
     def back_lanes(source):
         return pl.ds(pl.multiple_of(LANE + block_of(source) * block, LANE), block)
 
@@ -416,6 +454,19 @@
         return carry
 
     lax.fori_loop(0, nc // 2, two_contracted, 0)
+    for which, end in ends:
+
+        @pl.when(mine == end)
+        def _(which=which):
+            relay(which).wait_recv()
+
+            def start_hand(off, carry):
+                hand(which, (me + off) % nb).start()
+                return carry
+
+            lax.fori_loop(1, nb, start_hand, 0)
+            keep(which).start()
+
     layers = [layer_buf[step] for step in range(nc // 2)]
     for matrix in (two_t, three_t):
         layers = [jnp.tanh(dot32(matrix[...], layer)).astype(jnp.bfloat16) for layer in layers]
@@ -456,27 +507,6 @@
         return carry
 
     lax.fori_loop(1, nb, wait_y, 0)
-
-    edges = [
-        pltpu.make_async_remote_copy(
-            src_ref=back.at[0, :, :, pl.ds(last, LANE)],
-            dst_ref=back.at[0, :, :, pl.ds(0, LANE)],
-            send_sem=edge_send.at[0],
-            recv_sem=edge_recv.at[0],
-            device_id=device(me, up),
-            device_id_type=MESH,
-        ),
-        pltpu.make_async_remote_copy(
-            src_ref=back.at[0, :, :, pl.ds(LANE, LANE)],
-            dst_ref=back.at[0, :, :, pl.ds(last + LANE, LANE)],
-            send_sem=edge_send.at[1],
-            recv_sem=edge_recv.at[1],
-            device_id=device(me, down),
-            device_id_type=MESH,
-        ),
-    ]
-    for edge in edges:
-        edge.start()
 
     def one_tile(tile, carry):
         at = [pl.ds(pl.multiple_of((tile + k) * LANE, LANE), LANE) for k in range(3)]
@@ -507,8 +537,16 @@
         return carry
 
     lax.fori_loop(0, (tiles - 2) // together, inner_tiles, 0)
-    for edge in edges:
-        edge.wait_recv()
+    for which, end in ends:
+
+        @pl.when(mine == end)
+        def _(which=which):
+            keep(which).wait()
+
+        @pl.when(mine != end)
+        def _(which=which):
+            hand(which, me).wait_recv()
+
 
     def outer_tile(which, carry):
         return one_tile(which * (tiles - 1), carry)
@@ -535,8 +573,21 @@
         return carry
 
     lax.fori_loop(1, nb, drain, 0)
-    for copy in halos + edges:
-        copy.wait_send()
+    for halo in halos:
+        halo.wait_send()
+    for which, end in ends:
+
+        @pl.when(mine == nb - 1 - end)
+        def _(which=which):
+            relay(which).wait_send()
+
+        @pl.when(mine == end)
+        def _(which=which):
+            def drain_hand(off, carry):
+                hand(which, (me + off) % nb).wait_send()
+                return carry
+
+            lax.fori_loop(1, nb, drain_hand, 0)
 
 
 def body(
@@ -600,6 +651,7 @@
             pltpu.VMEM((NC // 2, 3, 2 * block), f32),
             pltpu.VMEM((nb, 3, bl, block), f32),
             pltpu.VMEM((3, bl, atoms), f32),
+            pltpu.VMEM((2, nb, 3, bl, LANE), f32),
             pltpu.VMEM((3, bl, atoms), f32),
             pltpu.VMEM((width, atoms), jnp.int32),
             pltpu.VMEM((wide, env), bf16),
@@ -610,7 +662,7 @@
             pltpu.VMEM((NC // 2, env, 2 * block), bf16),
             pltpu.VMEM((NC // 2, hid, 2 * block), bf16),
             dma((16,)),
-            dma((3,)),
+            dma((5,)),
             dma((nb,)),
             dma((nb,)),
             dma((nb,)),
@@ -618,6 +670,8 @@
             dma((nb,)),
             dma((nb,)),
             dma((2,)),
+            dma((2,)),
+            dma((nb,)),
             dma((2,)),
             dma((2,)),
             dma((2,)),

time: 46 us -> 45 us (0.978)
  the two profiles are of different devices: /device:TPU:1 before, /device:TPU:0 now
where the time goes in v4:
time: 45 us; the launch traced here: 44.9 us
  Pallas kernels  42.2 us (94%)
  local copies, waits for them, and re-layouts  2.03 us (5%)
  between operations  0.64 us (1%)
    pallas_call x1, Pallas kernels, body(): pl.pallas_call(functools.partial(kernel, nb), out_shape=(out, out, out),...  42.2 us
    unnamed x3, local copies, waits for them, and re-layouts  2.03 us

profile of v4, /device:TPU:0, one launch (start us, length us, event | category | flops | bytes accessed | tf_op | source)
XLA Modules:
  0.0 44.9 jit_solution(10815575252258130512)
XLA Ops:
  0.6 42.2 %shard_map.157 = (f32[3,4,4096]{2,1,0:T(4,128)S(1)}, f32[3,4,4096]{2,1,0:T(4,128)S(1)}, f32[3,4,4096]{2,1,0:T(4,128)S(1)}) custom-call(f32[3,4,4096]{2,1,0:T(4,128)} %bitcast.18, f32[3,4,4096]{2,1,0:T(4,128)} %bitcast.19, f32[3,4,4096]{2,1,0:T(4,128)} %bitcast.20, f32[3,4,4096]{2,1,0:T(4,128)} %bitcast.21, f32[32,128]{1,0:T(8,128)} %bitcast.22, ...), custom_call_target="tpu_custom_call" | custom-call | tf_op jit(solution)/shard_map/pallas_call | solution.py:628
  42.9 0.7 %copy.20 = f32[4,3,4096]{2,0,1:T(4,128)} copy(f32[4,3,4096]{2,0,1:T(4,128)S(1)} %bitcast.14) | data formatting | bytes 393216
  43.5 0.7 %copy.21 = f32[4,3,4096]{2,0,1:T(4,128)} copy(f32[4,3,4096]{2,0,1:T(4,128)S(1)} %bitcast.13) | data formatting | bytes 393216
  44.2 0.7 %copy.22 = f32[4,3,4096]{2,0,1:T(4,128)} copy(f32[4,3,4096]{2,0,1:T(4,128)S(1)} %bitcast.12) | data formatting | bytes 393216

commit v5 on v4

--- a/solution.py
+++ b/solution.py
@@ -246,8 +246,6 @@
         pltpu.make_async_copy(source, dest, local_sem.at[at])
         for at, (source, dest) in enumerate(moves)
     ]
-    for load in loads:
-        load.start()
 
     barrier = pltpu.get_barrier_semaphore()
 
@@ -260,6 +258,8 @@
     lax.fori_loop(1, nb, greet, 0)
     for other in (before, after):
         pl.semaphore_signal(barrier, inc=1, device_id=other, device_id_type=MESH)
+    for load in loads:
+        load.start()
     for load in loads[:4]:
         load.wait()
     sent[1] = p_ref[...] + 0.5 * TIME_STEP * f_ref[...]
@@ -442,18 +442,18 @@
     chunk = 512
     depth = one.shape[1]
 
-    def two_contracted(step, carry):
-        env = env_buf[step]
-        total_one = None
+    def all_contracted():
+        sums = [None] * 4
         for low_at in range(0, depth, chunk):
             high_at = min(low_at + chunk, depth)
-            piece = jnp.tanh(dot32(desc_p[low_at:high_at, :], env)).astype(jnp.bfloat16)
-            term = dot32(one[:, low_at:high_at], piece)
-            total_one = term if total_one is None else total_one + term
-        layer_buf[step] = jnp.tanh(total_one).astype(jnp.bfloat16)
-        return carry
-
-    lax.fori_loop(0, nc // 2, two_contracted, 0)
+            for k in range(4):
+                piece = jnp.tanh(dot32(desc_p[low_at:high_at, :], env_buf[k]))
+                term = dot32(one[:, low_at:high_at], piece.astype(jnp.bfloat16))
+                sums[k] = term if sums[k] is None else sums[k] + term
+        for k in range(4):
+            layer_buf[k] = jnp.tanh(sums[k]).astype(jnp.bfloat16)
+
+    all_contracted()
     for which, end in ends:
 
         @pl.when(mine == end)
@@ -529,7 +529,7 @@
             )
         return carry
 
-    together = next(n for n in (5, 3, 2, 1) if (tiles - 2) % n == 0)
+    together = next(n for n in (10, 5, 3, 2, 1) if (tiles - 2) % n == 0)
 
     def inner_tiles(step, carry):
         for k in range(together):

time: 45 us -> 43.6 us (0.969)
  Pallas kernels: 42.2 us -> 40.8 us
    pallas_call x1, Pallas kernels: 42.2 us -> 40.8 us  [body(): pl.pallas_call(functools.partial(kernel, nb), out_shape=(out, out, out),...]
where the time goes in v5:
time: 43.6 us; the launch traced here: 43.5 us
  Pallas kernels  40.8 us (94%)
  local copies, waits for them, and re-layouts  2.03 us (5%)
  between operations  0.64 us (1%)
    pallas_call x1, Pallas kernels, body(): pl.pallas_call(functools.partial(kernel, nb), out_shape=(out, out, out),...  40.8 us
    unnamed x3, local copies, waits for them, and re-layouts  2.03 us

profile of v5, /device:TPU:0, one launch (start us, length us, event | category | flops | bytes accessed | tf_op | source)
XLA Modules:
  0.0 43.5 jit_solution(7775813301420865817)
XLA Ops:
  0.6 40.8 %shard_map.157 = (f32[3,4,4096]{2,1,0:T(4,128)S(1)}, f32[3,4,4096]{2,1,0:T(4,128)S(1)}, f32[3,4,4096]{2,1,0:T(4,128)S(1)}) custom-call(f32[3,4,4096]{2,1,0:T(4,128)} %bitcast.18, f32[3,4,4096]{2,1,0:T(4,128)} %bitcast.19, f32[3,4,4096]{2,1,0:T(4,128)} %bitcast.20, f32[3,4,4096]{2,1,0:T(4,128)} %bitcast.21, f32[32,128]{1,0:T(8,128)} %bitcast.22, ...), custom_call_target="tpu_custom_call" | custom-call | tf_op jit(solution)/shard_map/pallas_call | solution.py:628
  41.4 0.7 %copy.20 = f32[4,3,4096]{2,0,1:T(4,128)} copy(f32[4,3,4096]{2,0,1:T(4,128)S(1)} %bitcast.14) | data formatting | bytes 393216
  42.1 0.7 %copy.21 = f32[4,3,4096]{2,0,1:T(4,128)} copy(f32[4,3,4096]{2,0,1:T(4,128)S(1)} %bitcast.13) | data formatting | bytes 393216
  42.8 0.7 %copy.22 = f32[4,3,4096]{2,0,1:T(4,128)} copy(f32[4,3,4096]{2,0,1:T(4,128)S(1)} %bitcast.12) | data formatting | bytes 393216

commit v6 on v5

--- a/solution.py
+++ b/solution.py
@@ -134,7 +134,8 @@
     s_low_hbm,
     out_q,
     out_m,
-    out_f,
+    pair_buf,
+    s_recv,
     p_ref,
     f_ref,
     mass_ref,
@@ -154,9 +155,7 @@
     ext,
     neural,
     s_buf,
-    s_recv,
     edge_buf,
-    pair_buf,
     lists,
     desc,
     desc_p,
@@ -553,23 +552,13 @@
 
     lax.fori_loop(0, 2, outer_tile, 0)
 
-    s_own.wait()
-
-    def wait_s(off, carry):
-        send_s((me + off) % nb, (me + off) % nb).wait_recv()
-        return carry
-
-    lax.fori_loop(1, nb, wait_s, 0)
-    force = pair_buf[...] + s_recv[...]
-    out_f[...] = force
-    out_m[...] = back[1, :, :, LANE : LANE + last] + 0.5 * TIME_STEP * force
     out_q[...] = back[0, :, :, LANE : LANE + last]
+    out_m[...] = back[1, :, :, LANE : LANE + last]
 
     def drain(off, carry):
         dest = (me + off) % nb
         send_in(dest, me).wait_send()
         send_y(dest, me).wait_send()
-        send_s(dest, me).wait_send()
         return carry
 
     lax.fori_loop(1, nb, drain, 0)
@@ -588,6 +577,20 @@
                 return carry
 
             lax.fori_loop(1, nb, drain_hand, 0)
+
+    s_own.wait()
+
+    def wait_s(off, carry):
+        send_s((me + off) % nb, (me + off) % nb).wait_recv()
+        return carry
+
+    lax.fori_loop(1, nb, wait_s, 0)
+
+    def drain_s(off, carry):
+        send_s((me + off) % nb, me).wait_send()
+        return carry
+
+    lax.fori_loop(1, nb, drain_s, 0)
 
 
 def body(
@@ -625,11 +628,11 @@
     out = jax.ShapeDtypeStruct((3, bl, atoms), jnp.float32)
     f32, bf16 = jnp.float32, jnp.bfloat16
     dma = pltpu.SemaphoreType.DMA
-    new_q, new_m, new_f = pl.pallas_call(
+    new_q, moved, pair, spread = pl.pallas_call(
         functools.partial(kernel, nb),
-        out_shape=(out, out, out),
+        out_shape=(out,) * 4,
         in_specs=[pl.BlockSpec(memory_space=pltpu.HBM)] * 16,
-        out_specs=(pl.BlockSpec(memory_space=pltpu.VMEM),) * 3,
+        out_specs=(pl.BlockSpec(memory_space=pltpu.VMEM),) * 4,
         scratch_shapes=[
             pltpu.VMEM((3, bl, atoms), f32),
             pltpu.VMEM((3, bl, atoms), f32),
@@ -650,9 +653,7 @@
             pltpu.VMEM((3, NC, 1, block + 2 * LANE), f32),
             pltpu.VMEM((NC // 2, 3, 2 * block), f32),
             pltpu.VMEM((nb, 3, bl, block), f32),
-            pltpu.VMEM((3, bl, atoms), f32),
             pltpu.VMEM((2, nb, 3, bl, LANE), f32),
-            pltpu.VMEM((3, bl, atoms), f32),
             pltpu.VMEM((width, atoms), jnp.int32),
             pltpu.VMEM((wide, env), bf16),
             pltpu.VMEM((wide, env), bf16),
@@ -698,7 +699,8 @@
         s_high,
         s_low,
         )])
-    return flip(new_q), flip(new_m), flip(new_f)
+    force = pair + spread
+    return flip(new_q), flip(moved + 0.5 * TIME_STEP * force), flip(force)
 
 
 def solution(mesh):

time: 43.6 us -> 43.2 us (level)
  local copies, waits for them, and re-layouts: 2.03 us -> 0.68 us
  other arithmetic: 0 us -> 0.84 us
    unnamed x3 -> x1, local copies, waits for them, and re-layouts: 2.03 us -> 0.68 us
    transpose x0 -> x1, other arithmetic: none -> 0.84 us  [flip(): return jnp.transpose(x, (1, 0, 2))]
where the time goes in v6:
time: 43.2 us; the launch traced here: 43.1 us
  Pallas kernels  40.9 us (95%)
  other arithmetic  0.84 us (2%)
  local copies, waits for them, and re-layouts  0.68 us (2%)
  between operations  0.64 us (1%)
    pallas_call x1, Pallas kernels, body(): pl.pallas_call(functools.partial(kernel, nb), out_shape=(out,) * 4, in_sp...  40.9 us

profile of v6, /device:TPU:0, one launch (start us, length us, event | category | flops | bytes accessed | tf_op | source)
XLA Modules:
  0.0 43.1 jit_solution(12691641022597438739)
XLA Ops:
  0.6 40.9 %shard_map.157 = (f32[3,4,4096]{2,1,0:T(4,128)S(1)}, f32[3,4,4096]{2,1,0:T(4,128)S(1)}, f32[3,4,4096]{2,1,0:T(4,128)S(1)}, f32[3,4,4096]{2,1,0:T(4,128)S(1)}) custom-call(f32[3,4,4096]{2,1,0:T(4,128)} %bitcast.18, f32[3,4,4096]{2,1,0:T(4,128)} %bitcast.19, f32[3,4,4096]{2,1,0:T(4,128)} %bitcast.20, f32[3,4,4096]{2,1,0:T(4,128)} %bitcast.21, ...), custom_call_target="tpu_custom_call" | custom-call | tf_op jit(solution)/shard_map/pallas_call | solution.py:631
  41.5 0.8 %add_bitcast_fusion.1 = (f32[4,3,4096]{2,0,1:T(4,128)}, f32[4,3,4096]{2,0,1:T(4,128)}) fusion(f32[3,4,4096]{2,1,0:T(4,128)S(1)} %get-tuple-element.9, f32[3,4,4096]{2,1,0:T(4,128)S(1)} %get-tuple-element.10, f32[3,4,4096]{2,1,0:T(4,128)S(1)} %get-tuple-element.8), kind=kLoop, calls=%fused_computation.1 | loop fusion | flops 147456 | bytes 983040 | tf_op jit(solution)/shard_map/transpose | solution.py:626
  42.4 0.7 %copy.18 = f32[4,3,4096]{2,0,1:T(4,128)} copy(f32[4,3,4096]{2,0,1:T(4,128)S(1)} %bitcast.14) | data formatting | bytes 393216
